TPU v7x, 32 devices: a whole 2x2x4 slice. The times are simulated.
32 devices in a mesh: seq: 8 (over y, x, core), batch: 4 (over z).
Axes of the slice: x: 2, y: 2, z: 4, core: 2. Of those that a mesh axis runs over, the one named last changes fastest.
Arguments:
- tokens: bfloat16 [16, 1024, 1152], P('batch', 'seq'), may hold values from -6 to 6
- condition: bfloat16 [16, 1152], P('batch'), may hold values from -6 to 6
- segment_ids: int32 [16, 1024], P('batch'), may hold values from 0 to 3, never falling along the last dimension, each value on 1 to 512 neighbouring positions
- cotangent: bfloat16 [16, 1024, 1152], P('batch', 'seq'), may hold values from -6 to 6
- block_slots: int32 [432], replicated, may hold values from 0 to 447, as said below
- modulator_slots: int32 [216], replicated, may hold values from 0 to 223, as said below
- block_low: bfloat16 [448, 32, 1152], P(('seq', 'batch')), may hold values from -0.1875 to 0.1875
- block_master: float32 [448, 32, 1152], P(('seq', 'batch')), may hold values from -0.1875 to 0.1875
- block_first: float32 [448, 32, 1152], P(('seq', 'batch')), may hold values from -0.015625 to 0.015625
- block_second: float32 [448, 32, 1152], P(('seq', 'batch')), may hold values from 5e-07 to 8e-06
- block_ema: float32 [448, 32, 1152], P(('seq', 'batch')), may hold values from -0.1875 to 0.1875
- modulator_low: bfloat16 [224, 32, 1152], P(('seq', 'batch')), may hold values from -0.1875 to 0.1875
- modulator_master: float32 [224, 32, 1152], P(('seq', 'batch')), may hold values from -0.1875 to 0.1875
- modulator_first: float32 [224, 32, 1152], P(('seq', 'batch')), may hold values from -0.015625 to 0.015625
- modulator_second: float32 [224, 32, 1152], P(('seq', 'batch')), may hold values from 5e-07 to 8e-06
- modulator_ema: float32 [224, 32, 1152], P(('seq', 'batch')), may hold values from -0.1875 to 0.1875
- biases: float32 [16128], replicated, may hold values from -4 to 4
- bias_first: float32 [16128], replicated, may hold values from -0.015625 to 0.015625
- bias_second: float32 [16128], replicated, may hold values from 5e-07 to 8e-06
- bias_ema: float32 [16128], replicated, may hold values from -4 to 4
Outputs:
- output: bfloat16 [16, 1024, 1152], P('batch', 'seq')
- tokens_grad: float32 [16, 1024, 1152], P('batch', 'seq')
- condition_grad: float32 [16, 1152], P('batch')
- block_grad: float32 [448, 32, 1152], P(('seq', 'batch'))
- block_new: float32 [448, 32, 1152], P(('seq', 'batch'))
- block_first_new: float32 [448, 32, 1152], P(('seq', 'batch'))
- block_second_new: float32 [448, 32, 1152], P(('seq', 'batch'))
- block_ema_new: float32 [448, 32, 1152], P(('seq', 'batch'))
- block_low_new: bfloat16 [448, 32, 1152], P(('seq', 'batch'))
- modulator_grad: float32 [224, 32, 1152], P(('seq', 'batch'))
- modulator_new: float32 [224, 32, 1152], P(('seq', 'batch'))
- modulator_first_new: float32 [224, 32, 1152], P(('seq', 'batch'))
- modulator_second_new: float32 [224, 32, 1152], P(('seq', 'batch'))
- modulator_ema_new: float32 [224, 32, 1152], P(('seq', 'batch'))
- modulator_low_new: bfloat16 [224, 32, 1152], P(('seq', 'batch'))
- bias_grad: float32 [16128], replicated
- biases_new: float32 [16128], replicated
- bias_first_new: float32 [16128], replicated
- bias_second_new: float32 [16128], replicated
- bias_ema_new: float32 [16128], replicated
Inputs may be any that keep to these rules, and one draw needn't show every extreme that they name: Distinct values; tile t lies in slot block_slots[t], held by device slot // 14 of seq+batch. Distinct values; tile t lies in slot modulator_slots[t], held by device slot // 7 of seq+batch. `segment_ids`: never falls along a sequence's tokens.
All inputs are finite; a program needn't handle non-finite values.
Results may differ from a plain program's by a relative error of at most 0.015.
The roundings to bfloat16 on the way count: a program that leaves them out, or rounds other values in their place, can miss the bound.
Values may be sent and summed in bfloat16 or wider, within the bound.
No kernel may reach another device: no remote copies, remote signals or barrier semaphores. Data moves between devices by JAX's collectives and lax.ppermute only.
A program may use at most 384 MiB of HBM per device.

v0:
```python
import jax
import jax.numpy as jnp
from jax import lax
from jax.sharding import PartitionSpec as P

D = 1152
HEADS = 16
HD = 72
FF = 4608
F = 16
PPD = 8
TR = 32
STEP = 5
NT_W = 432
NT_A = 216


ln_eps = 1e-06
adam_eps = 1e-08
beta_one = 0.5
beta_two = 0.5
learn_rate = 0.01
bias_rate = 0.1
decay_rate = 0.1
ema_rate = 0.9
clip_rms = 0.001
highest = lax.Precision.HIGHEST


def contract_last(left, right):
    return lax.dot_general(
        left, right, (((left.ndim - 1,), (1,)), ((), ())), preferred_element_type=jnp.float32
    )


def contract_first(left, right):
    return lax.dot_general(
        left, right, (((left.ndim - 1,), (0,)), ((), ())), preferred_element_type=jnp.float32
    )


def token_outer(grads, values):
    leading = tuple(range(grads.ndim - 1))
    return lax.dot_general(
        grads, values, ((leading, leading), ((), ())), preferred_element_type=jnp.float32
    )


def norm_rows(values):
    center = values - jnp.mean(values, axis=-1, keepdims=True)
    factor = lax.rsqrt(jnp.mean(center * center, axis=-1, keepdims=True) + ln_eps)
    return (center * factor, factor)


def norm_back(normed, factor, grads):
    return factor * (
        grads
        - jnp.mean(grads, axis=-1, keepdims=True)
        - normed * jnp.mean(grads * normed, axis=-1, keepdims=True)
    )


def swish(values):
    return values * jax.nn.sigmoid(values)


def gelu_tanh(values):
    return jax.nn.gelu(values, approximate=True)


def slope_of(function, values):
    return jax.vjp(function, values)[1](jnp.ones_like(values))[0]


def slot_rows(terms, owners):
    rows = jnp.take(terms, jnp.maximum(owners, 0), axis=0)
    return rows * (owners >= 0).astype(jnp.float32)[:, None, None]


def clip_factor(square_sum, count):
    return jnp.minimum(1.0, clip_rms * lax.rsqrt(square_sum / count + 1e-12))


def adam_rule(grads, clip, master, first, second, ema_old, live, rate):
    used = grads * clip
    first_new = beta_one * first + (1.0 - beta_one) * used
    second_new = beta_two * second + (1.0 - beta_two) * used * used
    fix_one = 1.0 - beta_one**STEP
    fix_two = 1.0 - beta_two**STEP
    step_size = rate * (
        first_new / fix_one / (jnp.sqrt(second_new / fix_two) + adam_eps) + decay_rate * master
    )
    master_new = master - step_size
    ema_new = ema_rate * ema_old + (1.0 - ema_rate) * master_new
    return (
        grads * live,
        master_new * live,
        first_new * live,
        second_new * live,
        ema_new * live,
        (master_new * live).astype(jnp.bfloat16),
    )


def on_device(
    tokens,
    condition,
    segment_ids,
    cotangent,
    block_slots,
    modulator_slots,
    block_low,
    block_master,
    block_first,
    block_second,
    block_ema,
    modulator_low,
    modulator_master,
    modulator_first,
    modulator_second,
    modulator_ema,
    biases,
    bias_first,
    bias_second,
    bias_ema,
):
    seq_local = tokens.shape[0]
    frame_rows = tokens.shape[1]
    groups = lax.axis_size("seq")
    pair_local = frame_rows // groups
    device_count = lax.axis_size(("seq", "batch"))
    device_place = lax.axis_index(("seq", "batch"))
    block_local = block_low.shape[0]
    modul_local = modulator_low.shape[0]
    tile_of_block = (
        jnp.full((block_local * device_count,), -1, jnp.int32)
        .at[block_slots]
        .set(jnp.arange(NT_W, dtype=jnp.int32))
    )
    tile_of_modul = (
        jnp.full((modul_local * device_count,), -1, jnp.int32)
        .at[modulator_slots]
        .set(jnp.arange(NT_A, dtype=jnp.int32))
    )
    gathered_block, gathered_modul = (
        lax.all_gather(block_low, ("seq", "batch"), axis=0, tiled=True),
        lax.all_gather(modulator_low, ("seq", "batch"), axis=0, tiled=True),
    )
    block_rows = jnp.take(gathered_block, block_slots, axis=0).reshape(NT_W * TR, D)
    w_qkv = block_rows[: 3 * D]
    w_out = block_rows[3 * D : 4 * D]
    w_up = block_rows[4 * D : 4 * D + FF]
    w_down = block_rows[4 * D + FF :]
    w_modul = jnp.take(gathered_modul, modulator_slots, axis=0).reshape(6 * D, D)
    b_modul = biases[: 6 * D]
    b_query = biases[6 * D : 7 * D]
    b_value = biases[7 * D : 8 * D]
    b_out = biases[8 * D : 9 * D]
    b_up = biases[9 * D : 9 * D + FF]
    b_down = biases[9 * D + FF :]
    cond_float = condition.astype(jnp.float32)
    cond_low = swish(cond_float).astype(jnp.bfloat16)
    modul = contract_last(cond_low, w_modul) + b_modul
    shift_one, scale_one, gate_one, shift_two, scale_two, gate_two = [
        piece[:, None, :] for piece in jnp.split(modul, 6, axis=1)
    ]
    x_float = tokens.astype(jnp.float32)
    normed_one, factor_one = norm_rows(x_float)
    act_one = (normed_one * (1.0 + scale_one) + shift_one).astype(jnp.bfloat16)
    patch_one = lax.all_to_all(
        act_one.reshape(seq_local, pair_local, groups, D),
        "seq",
        split_axis=2,
        concat_axis=1,
        tiled=True,
    ).reshape(seq_local, F, PPD, D)
    ids_patch = lax.dynamic_index_in_dim(
        segment_ids.reshape(seq_local, F, PPD, groups),
        lax.axis_index("seq"),
        axis=3,
        keepdims=False,
    )
    ids_order = jnp.transpose(ids_patch, (0, 2, 1))
    same_seg = (ids_order[:, :, :, None] == ids_order[:, :, None, :])[:, :, None]
    qkv_bias = jnp.concatenate([b_query, jnp.zeros((D,), jnp.float32), b_value])
    qkv = contract_last(patch_one, w_qkv) + qkv_bias
    head_shape = (seq_local, F, PPD, HEADS, HD)
    query = qkv[..., :D].astype(jnp.bfloat16).reshape(head_shape)
    keyed = qkv[..., D : 2 * D].astype(jnp.bfloat16).reshape(head_shape)
    valued = qkv[..., 2 * D :].astype(jnp.bfloat16).reshape(head_shape)
    score_scale = HD ** (-0.5)
    scores = (
        jnp.einsum("sfphd,sgphd->sphfg", query, keyed, preferred_element_type=jnp.float32)
        * score_scale
    )
    masked = jnp.where(same_seg, scores, -1e30)
    exps = jnp.exp(masked - jnp.max(masked, axis=-1, keepdims=True))
    probs = exps / jnp.sum(exps, axis=-1, keepdims=True)
    probs_low = probs.astype(jnp.bfloat16)
    attended = jnp.einsum(
        "sphfg,sgphd->sfphd", probs_low, valued, preferred_element_type=jnp.float32
    )
    attended = attended.reshape(seq_local, F, PPD, D).astype(jnp.bfloat16)
    attention_low = (contract_last(attended, w_out) + b_out).astype(jnp.bfloat16)
    frames_attention = lax.all_to_all(
        attention_low.reshape(seq_local, frame_rows, 1, D),
        "seq",
        split_axis=1,
        concat_axis=2,
        tiled=True,
    ).reshape(seq_local, frame_rows, D)
    attention_float = frames_attention.astype(jnp.float32)
    middle = x_float + gate_one * attention_float
    normed_two, factor_two = norm_rows(middle)
    act_two = (normed_two * (1.0 + scale_two) + shift_two).astype(jnp.bfloat16)
    pre_up = contract_last(act_two, w_up) + b_up
    gelu_low = gelu_tanh(pre_up).astype(jnp.bfloat16)
    down = contract_first(gelu_low, w_down) + b_down
    output = (middle + gate_two * down).astype(jnp.bfloat16)
    d_out = cotangent.astype(jnp.float32)
    d_down = (gate_two * d_out).astype(jnp.bfloat16)
    grad_gate_two = jnp.sum(d_out * down, axis=1)
    grad_w_down = token_outer(gelu_low, d_down)
    bias_down = jnp.sum(d_down.astype(jnp.float32), axis=(0, 1))
    d_gelu = contract_last(d_down, w_down)
    d_pre = (d_gelu * slope_of(gelu_tanh, pre_up)).astype(jnp.bfloat16)
    grad_w_up = token_outer(d_pre, act_two)
    bias_up = jnp.sum(d_pre.astype(jnp.float32), axis=(0, 1))
    d_act_two = contract_first(d_pre, w_up)
    grad_shift_two = jnp.sum(d_act_two, axis=1)
    grad_scale_two = jnp.sum(d_act_two * normed_two, axis=1)
    d_middle = d_out + norm_back(normed_two, factor_two, d_act_two * (1.0 + scale_two))
    d_attention = (gate_one * d_middle).astype(jnp.bfloat16)
    grad_gate_one = jnp.sum(d_middle * attention_float, axis=1)
    patch_d_attention = lax.all_to_all(
        d_attention.reshape(seq_local, pair_local, groups, D),
        "seq",
        split_axis=2,
        concat_axis=1,
        tiled=True,
    ).reshape(seq_local, F, PPD, D)
    grad_w_out = token_outer(patch_d_attention, attended)
    bias_out = jnp.sum(patch_d_attention.astype(jnp.float32), axis=(0, 1, 2))
    d_attended = contract_first(patch_d_attention, w_out).astype(jnp.bfloat16).reshape(head_shape)
    d_probs = jnp.einsum(
        "sfphd,sgphd->sphfg", d_attended, valued, preferred_element_type=jnp.float32
    )
    d_value = jnp.einsum(
        "sphfg,sfphd->sgphd", probs_low, d_attended, preferred_element_type=jnp.float32
    )
    d_scores = (probs * (d_probs - jnp.sum(probs * d_probs, axis=-1, keepdims=True))).astype(
        jnp.bfloat16
    )
    d_query = (
        jnp.einsum("sphfg,sgphd->sfphd", d_scores, keyed, preferred_element_type=jnp.float32)
        * score_scale
    )
    d_key = (
        jnp.einsum("sphfg,sfphd->sgphd", d_scores, query, preferred_element_type=jnp.float32)
        * score_scale
    )
    flat_shape = (seq_local, F, PPD, D)
    d_qkv = jnp.concatenate(
        [d_query.reshape(flat_shape), d_key.reshape(flat_shape), d_value.reshape(flat_shape)],
        axis=-1,
    ).astype(jnp.bfloat16)
    grad_w_qkv = token_outer(d_qkv, patch_one)
    d_qkv_float = d_qkv.astype(jnp.float32)
    bias_query = jnp.sum(d_qkv_float[..., :D], axis=(0, 1, 2))
    bias_value = jnp.sum(d_qkv_float[..., 2 * D :], axis=(0, 1, 2))
    d_act_one = contract_first(d_qkv, w_qkv).astype(jnp.bfloat16)
    frames_d_act = (
        lax.all_to_all(
            d_act_one.reshape(seq_local, frame_rows, 1, D),
            "seq",
            split_axis=1,
            concat_axis=2,
            tiled=True,
        )
        .reshape(seq_local, frame_rows, D)
        .astype(jnp.float32)
    )
    grad_shift_one = jnp.sum(frames_d_act, axis=1)
    grad_scale_one = jnp.sum(frames_d_act * normed_one, axis=1)
    tokens_grad = d_middle + norm_back(normed_one, factor_one, frames_d_act * (1.0 + scale_one))
    d_modul = jnp.concatenate(
        [
            grad_shift_one,
            grad_scale_one,
            grad_gate_one,
            grad_shift_two,
            grad_scale_two,
            grad_gate_two,
        ],
        axis=1,
    )
    cond_slope = slope_of(swish, cond_float)
    w_modul_float = w_modul.astype(jnp.float32)
    cond_low_float = cond_low.astype(jnp.float32)
    cond_term = jnp.dot(d_modul, w_modul_float, precision=highest) * cond_slope
    condition_grad = lax.psum(cond_term, "seq")
    modul_terms = jnp.dot(d_modul.T, cond_low_float, precision=highest).reshape(NT_A, TR, D)
    modulator_grad = lax.psum_scatter(
        slot_rows(modul_terms, tile_of_modul), ("seq", "batch"), scatter_dimension=0, tiled=True
    )
    block_terms = jnp.concatenate([grad_w_qkv, grad_w_out, grad_w_up, grad_w_down], axis=0).reshape(
        NT_W, TR, D
    )
    block_grad = lax.psum_scatter(
        slot_rows(block_terms, tile_of_block), ("seq", "batch"), scatter_dimension=0, tiled=True
    )
    bias_terms = jnp.concatenate(
        [jnp.sum(d_modul, axis=0), bias_query, bias_value, bias_out, bias_up, bias_down]
    )
    bias_grad = lax.psum(bias_terms, ("seq", "batch"))
    block_square, modul_square = lax.psum(
        (jnp.sum(block_grad * block_grad), jnp.sum(modulator_grad * modulator_grad)),
        ("seq", "batch"),
    )
    clip_block = clip_factor(block_square, float(NT_W * TR * D))
    clip_modul = clip_factor(modul_square, float(NT_A * TR * D))
    clip_bias = clip_factor(jnp.sum(bias_grad * bias_grad), float(bias_grad.shape[0]))
    block_mine = lax.dynamic_slice_in_dim(tile_of_block, device_place * block_local, block_local)
    block_live = (block_mine >= 0).astype(jnp.float32)[:, None, None]
    modul_mine = lax.dynamic_slice_in_dim(tile_of_modul, device_place * modul_local, modul_local)
    modul_live = (modul_mine >= 0).astype(jnp.float32)[:, None, None]
    blk = adam_rule(
        block_grad,
        clip_block,
        block_master,
        block_first,
        block_second,
        block_ema,
        block_live,
        learn_rate,
    )
    mdl = adam_rule(
        modulator_grad,
        clip_modul,
        modulator_master,
        modulator_first,
        modulator_second,
        modulator_ema,
        modul_live,
        learn_rate,
    )
    bia = adam_rule(bias_grad, clip_bias, biases, bias_first, bias_second, bias_ema, 1.0, bias_rate)
    return (
        output,
        tokens_grad,
        condition_grad,
        blk[0],
        blk[1],
        blk[2],
        blk[3],
        blk[4],
        blk[5],
        mdl[0],
        mdl[1],
        mdl[2],
        mdl[3],
        mdl[4],
        mdl[5],
        bia[0],
        bia[1],
        bia[2],
        bia[3],
        bia[4],
    )


def solution(mesh):
    placed = (
        P("batch", "seq", None),
        P("batch", None),
        P("batch", None),
        P("batch", "seq", None),
        P(),
        P(),
        P(("seq", "batch"), None, None),
        P(("seq", "batch"), None, None),
        P(("seq", "batch"), None, None),
        P(("seq", "batch"), None, None),
        P(("seq", "batch"), None, None),
        P(("seq", "batch"), None, None),
        P(("seq", "batch"), None, None),
        P(("seq", "batch"), None, None),
        P(("seq", "batch"), None, None),
        P(("seq", "batch"), None, None),
        P(),
        P(),
        P(),
        P(),
    )
    return jax.shard_map(
        on_device,
        mesh=mesh,
        in_specs=placed,
        out_specs=(
            P("batch", "seq", None),
            P("batch", "seq", None),
            P("batch", None),
            P(("seq", "batch"), None, None),
            P(("seq", "batch"), None, None),
            P(("seq", "batch"), None, None),
            P(("seq", "batch"), None, None),
            P(("seq", "batch"), None, None),
            P(("seq", "batch"), None, None),
            P(("seq", "batch"), None, None),
            P(("seq", "batch"), None, None),
            P(("seq", "batch"), None, None),
            P(("seq", "batch"), None, None),
            P(("seq", "batch"), None, None),
            P(("seq", "batch"), None, None),
            P(),
            P(),
            P(),
            P(),
            P(),
        ),
        check_vma=False,
    )
```

profile of v0, /device:TPU:0, one launch (start us, length us, event | category | flops | bytes accessed | tf_op | source)
XLA Modules:
  0.0 1702.7 jit_solution(11930538815193650629)
XLA Ops:
  13.3 113.7 %all-gather.3.cloned.1.call-done = bf16[224,32,1152]{2,1,0:T(8,128)(2,1)} async-done(((bf16[7,32,1152]{2,1,0:T(8,128)(2,1)}), bf16[224,32,1152]{2,1,0:T(8,128)(2,1)}) %all-gather.3.cloned.1.call-update) | async-done | bytes 16515088 | tf_op jit(solution)/shard_map/all_gather | solution.py:147
  126.9 15.7 gather_fusion
  142.6 14.5 bitcast_select_fusion
  157.1 9.7 convolution_add_fusion
  177.0 26.6 %all-to-all-done = bf16[4,16,8,1152]{3,1,0,2:T(8,128)(2,1)S(1)} async-done(((bf16[4,16,8,1152]{3,1,0,2:T(8,128)(2,1)}), bf16[4,16,8,1152]{3,1,0,2:T(8,128)(2,1)S(1)}, u32[]{:S(2)}, u32[]{:S(2)}) %all-to-all-start) | async-done | bytes 1179680 | tf_op jit(solution)/shard_map/all_to_all | solution.py:170
  203.7 128.6 %all-gather.5.cloned.1.call-done = bf16[448,32,1152]{2,1,0:T(8,128)(2,1)} async-done(((bf16[14,32,1152]{2,1,0:T(8,128)(2,1)}), bf16[448,32,1152]{2,1,0:T(8,128)(2,1)}) %all-gather.5.cloned.1.call-update) | async-done | bytes 33030160 | tf_op jit(solution)/shard_map/all_gather | solution.py:146
  332.4 23.8 %gather_fusion.1 = bf16[432,32,1152]{2,1,0:T(8,128)(2,1)} fusion(bf16[448,32,1152]{2,1,0:T(8,128)(2,1)} %all-gather.5.cloned.1.call-done, s32[1024]{0:T(1024)} %pad_clamp_fusion.2), kind=kCustom, calls=%fused_computation.1 | custom fusion | bytes 63702720 | tf_op jit(solution)/shard_map/jit(_take)/gather | solution.py:149
  356.2 21.8 %broadcast_select_fusion = bf16[432,32,1152]{2,1,0:T(8,128)(2,1)} fusion(bf16[432,32,1152]{2,1,0:T(8,128)(2,1)} %gather_fusion.1, pred[432]{0:T(512)(128)(4,1)S(1)} %copy-done.76), kind=kLoop, calls=%fused_computation.10 | loop fusion | flops 15925248 | bytes 63701424 | tf_op jit(solution)/shard_map/jit(_take)/select_n | solution.py:149
  381.5 7.1 slice.87
  388.5 8.4 add_convert_fusion
  441.1 16.1 fusion.78
  462.0 14.0 fusion.64
  476.1 15.5 convert_reduce_fusion
  491.6 13.6 multiply_reduce_fusion.1
  505.2 14.6 convert_reduce_fusion.2
  533.3 10.5 all-to-all-done.2
  550.8 6.1 reshape.218
  592.1 8.7 fusion.17
  607.1 14.0 convolution_bitcast_fusion.1
  628.6 18.5 %fusion.71 = f32[6912,1152]{1,0:T(8,128)} fusion(f32[4,6912]{1,0:T(4,128)S(1)} %constant_dynamic-update-slice_fusion.3, bf16[4,1152]{1,0:T(4,128)(2,1)S(1)} %copy-done.43), kind=kOutput, calls=%fused_computation.194 | convolution fusion | flops 382233600 | bytes 31970304 | tf_op jit(solution)/shard_map/dot_general | solution.py:302
  647.2 25.2 %gather_fusion.3 = f32[224,32,1152]{2,1,0:T(8,128)} fusion(f32[216,32,1152]{2,1,0:T(8,128)} %bitcast.131, s32[1024]{0:T(1024)S(1)} %get-tuple-element.86), kind=kCustom, calls=%fused_computation.3 | custom fusion | bytes 66061184 | tf_op jit(solution)/shard_map/jit(_take)/gather | solution.py:76
  672.4 23.8 %select_multiply_fusion.1 = f32[224,32,1152]{2,1,0:T(8,128)} fusion(f32[224,32,1152]{2,1,0:T(8,128)} %gather_fusion.3, f32[224]{0:T(256)S(1)} %copy-done.75, pred[224]{0:T(512)(128)(4,1)S(1)} %copy-done.82), kind=kLoop, calls=%fused_computation.9 | loop fusion | flops 16515072 | bytes 66061408 | tf_op jit(solution)/shard_map/mul | solution.py:77
  697.5 17.6 %convolution_bitcast_fusion = f32[4608,1152]{1,0:T(8,128)} fusion(bf16[4,128,1152]{2,1,0:T(8,128)(2,1)S(1)} %copy-done.84, f32[4,1152]{1,0:T(4,128)S(1)} %copy-done.58, f32[4,128,4608]{2,1,0:T(8,128)} %fusion.64, f32[4608]{0:T(1024)S(1)} %copy-done.56), kind=kOutput, calls=%fused_computation.11 | convolution fusion | flops 5461180416 | bytes 31887360 | tf_op jit(solution)/shard_map/dot_general | solution.py:44
  719.6 11.1 convolution_bitcast_fusion.2
  734.8 53.2 %pad_maximum_fusion = f32[13824,1152]{1,0:T(8,128)} fusion(f32[4608,1152]{1,0:T(8,128)} %convolution_bitcast_fusion, f32[4608,1152]{1,0:T(8,128)S(1)} %copy-done.4, f32[1152,1152]{1,0:T(8,128)} %convolution_bitcast_fusion.3, f32[3456,1152]{1,0:T(8,128)} %convolution_bitcast_fusion.2), kind=kLoop, calls=%fused_computation.8 | loop fusion | flops 47775744 | bytes 127401984 | tf_op jit(solution)/shard_map/concatenate | solution.py:306
  788.0 46.3 %gather_fusion.2 = f32[448,32,1152]{2,1,0:T(8,128)} fusion(f32[432,32,1152]{2,1,0:T(8,128)} %bitcast.130, s32[1024]{0:T(1024)S(1)} %copy-done.66), kind=kCustom, calls=%fused_computation.2 | custom fusion | bytes 132122368 | tf_op jit(solution)/shard_map/jit(_take)/gather | solution.py:76
  834.3 44.2 %select_multiply_fusion = f32[448,32,1152]{2,1,0:T(8,128)} fusion(f32[448,32,1152]{2,1,0:T(8,128)} %gather_fusion.2, f32[448]{0:T(512)S(1)} %copy-done.67, pred[448]{0:T(512)(128)(4,1)S(1)} %copy-done.81), kind=kLoop, calls=%fused_computation.7 | loop fusion | flops 33030144 | bytes 132122816 | tf_op jit(solution)/shard_map/mul | solution.py:77
  902.2 9.4 convolution_multiply_fusion
  911.6 100.8 %reduce-scatter.5.cloned.1.call-done = f32[7,32,1152]{2,1,0:T(8,128)} async-done(((f32[224,32,1152]{2,1,0:T(8,128)}), f32[7,32,1152]{2,1,0:T(8,128)}) %reduce-scatter.5.cloned.1.call-update) | async-done | bytes 1032208 | tf_op jit(solution)/shard_map/reduce_scatter | solution.py:303
  1014.6 597.0 %reduce-scatter.3.cloned.1.call-done = f32[14,32,1152]{2,1,0:T(8,128)} async-done(((f32[448,32,1152]{2,1,0:T(8,128)}), f32[14,32,1152]{2,1,0:T(8,128)}) %reduce-scatter.3.cloned.1.call-update) | async-done | bytes 2064400 | tf_op jit(solution)/shard_map/reduce_scatter | solution.py:309
  1614.3 23.9 %psum.28 = f32[4,1152]{1,0:T(4,128)} all-reduce(f32[4,1152]{1,0:T(4,128)S(1)} %convolution_multiply_fusion), channel_id=1, replica_groups=mesh['seq'=8,'batch'=4] {'seq'}, use_global_device_ids=true, to_apply=%region_17.18 | all-reduce | flops 4608 | bytes 36864 | tf_op jit(solution)/shard_map/psum | solution.py:301
  1638.2 40.1 %all-reduce = (f32[]{:T(128)}, f32[]{:T(128)}, f32[16128]{0:T(1024)S(1)}) all-reduce(f32[]{:T(128)} %multiply_reduce_fusion.6, f32[]{:T(128)} %multiply_reduce_fusion.7, f32[16128]{0:T(1024)S(1)} %copy-done.47), channel_id=1, replica_groups=mesh['seq'=8,'batch'=4] {'seq','batch'}, use_global_device_ids=true, to_apply=%region_21.22 | all-reduce | flops 16130 | bytes 129040 | tf_op jit(solution)/shard_map/psum | solution.py:316
  (299 shorter events, 191.6 us)
Async XLA Ops:
  7.2 119.7 %all-gather.3.cloned.1.call-start = ((), (), s32[]{:S(2)}) async-start(), calls=%async_computation.6 | async-start | bytes 17031168 | tf_op jit(solution)/shard_map/all_gather | solution.py:147
  7.9 324.4 %all-gather.5.cloned.1.call-start = ((), (), s32[]{:S(2)}) async-start(), calls=%async_computation.7 | async-start | bytes 34062336 | tf_op jit(solution)/shard_map/all_gather | solution.py:146
  12.8 154.7 %copy-start.51 = (f32[4,128]{1,0:T(4,128)}, f32[4,128]{1,0:T(4,128)S(1)}, u32[]{:S(2)}) copy-start(f32[4,128]{1,0:T(4,128)S(1)} %broadcast_multiply_fusion.13) | copy-start | bytes 6148
  13.3 154.2 %copy-start.53 = (f32[4,128]{1,0:T(4,128)}, f32[4,128]{1,0:T(4,128)S(1)}, u32[]{:S(2)}) copy-start(f32[4,128]{1,0:T(4,128)S(1)} %add_rsqrt_fusion.1) | copy-start | bytes 6148
  170.1 33.5 %all-to-all-start = ((bf16[4,16,8,1152]{3,1,0,2:T(8,128)(2,1)}), bf16[4,16,8,1152]{3,1,0,2:T(8,128)(2,1)S(1)}, u32[]{:S(2)}, u32[]{:S(2)}) async-start(bf16[4,16,8,1152]{3,1,0,2:T(8,128)(2,1)} %copy.111), calls=%async_computation | async-start | bytes 2359296 | tf_op jit(solution)/shard_map/all_to_all | solution.py:170
  203.7 184.8 %copy-start.29 = (bf16[4,8,16,1,1152]{4,2,1,0,3:T(8,128)(2,1)}, bf16[4,8,16,1,1152]{4,2,1,0,3:T(8,128)(2,1)S(1)}, u32[]{:S(2)}) copy-start(bf16[4,8,16,1,1152]{4,2,1,0,3:T(8,128)(2,1)S(1)} %copy.112) | copy-start | bytes 3538948
  203.7 152.4 %copy-start.76 = (pred[432]{0:T(512)(128)(4,1)S(1)}, pred[432]{0:T(512)(128)(4,1)}, u32[]{:S(2)}) copy-start(pred[432]{0:T(512)(128)(4,1)} %compare_and_fusion) | copy-start | bytes 1300
  436.9 21.1 %all-to-all-start.1 = ((bf16[4,128,1,1152]{3,0,2,1:T(4,128)(2,1)}), bf16[4,128,1,1152]{3,0,2,1:T(4,128)(2,1)}, u32[]{:S(2)}, u32[]{:S(2)}) async-start(bf16[4,128,1,1152]{3,0,2,1:T(4,128)(2,1)} %copy.119), calls=%async_computation.1 | async-start | bytes 2359296 | tf_op jit(solution)/shard_map/all_to_all | solution.py:205
  461.2 14.8 copy-start.6
  461.3 14.8 slice-start
  461.7 43.5 %copy-start.79 = (f32[4,128]{1,0:T(4,128)}, f32[4,128]{1,0:T(4,128)S(1)}, u32[]{:S(2)}) copy-start(f32[4,128]{1,0:T(4,128)S(1)} %add_rsqrt_fusion) | copy-start | bytes 6148
  522.8 21.1 %all-to-all-start.2 = ((bf16[4,16,8,1152]{3,1,0,2:T(8,128)(2,1)}), bf16[4,16,8,1152]{3,1,0,2:T(8,128)(2,1)}, u32[]{:S(2)}, u32[]{:S(2)}) async-start(bf16[4,16,8,1152]{3,1,0,2:T(8,128)(2,1)} %copy.121), calls=%async_computation.2 | async-start | bytes 2359296 | tf_op jit(solution)/shard_map/all_to_all | solution.py:235
  528.4 22.4 %copy-start.73 = (s32[224]{0:T(256)}, s32[224]{0:T(256)S(1)}, u32[]{:S(2)}) copy-start(s32[224]{0:T(256)S(1)} %scatter_custom_fusion.1) | copy-start | bytes 2692
  531.5 19.3 %copy-start.61 = (s32[448]{0:T(512)}, s32[448]{0:T(512)S(1)}, u32[]{:S(2)}) copy-start(s32[448]{0:T(512)S(1)} %scatter_custom_fusion) | copy-start | bytes 5380
  602.7 21.1 %all-to-all-start.3 = ((bf16[4,128,1,1152]{3,0,2,1:T(4,128)(2,1)}), bf16[4,128,1,1152]{3,0,2,1:T(4,128)(2,1)}, u32[]{:S(2)}, u32[]{:S(2)}) async-start(bf16[4,128,1,1152]{3,0,2,1:T(4,128)(2,1)} %copy.132), calls=%async_computation.3 | async-start | bytes 2359296 | tf_op jit(solution)/shard_map/all_to_all | solution.py:273
  607.0 405.4 %reduce-scatter.5.cloned.1.call-start = ((), (), s32[]{:S(2)}) async-start(), calls=%async_computation.9 | async-start | bytes 34062336 | tf_op jit(solution)/shard_map/reduce_scatter | solution.py:303
  628.6 18.5 %copy-start.26 = (f32[4,6912]{1,0:T(4,128)}, f32[4,6912]{1,0:T(4,128)S(1)}, u32[]{:S(2)}) copy-start(f32[4,6912]{1,0:T(4,128)S(1)} %constant_dynamic-update-slice_fusion.3) | copy-start | bytes 331780
  647.2 25.2 %copy-start.75 = (f32[224]{0:T(256)S(1)}, f32[224]{0:T(256)}, u32[]{:S(2)}) copy-start(f32[224]{0:T(256)} %get-tuple-element.78) | copy-start | bytes 2692
  647.2 25.2 %copy-start.82 = (pred[224]{0:T(512)(128)(4,1)S(1)}, pred[224]{0:T(512)(128)(4,1)}, u32[]{:S(2)}) copy-start(pred[224]{0:T(512)(128)(4,1)} %get-tuple-element.77) | copy-start | bytes 676
  696.2 915.4 %reduce-scatter.3.cloned.1.call-start = ((), (), s32[]{:S(2)}) async-start(), calls=%async_computation.8 | async-start | bytes 68124672 | tf_op jit(solution)/shard_map/reduce_scatter | solution.py:309
  697.5 17.6 %copy-start.28 = (bf16[4,16,8,1152]{3,2,1,0:T(8,128)(2,1)S(1)}, bf16[4,16,8,1152]{3,2,1,0:T(8,128)(2,1)}, u32[]{:S(2)}) copy-start(bf16[4,16,8,1152]{3,2,1,0:T(8,128)(2,1)} %convert_element_type.132) | copy-start | bytes 3538948
  697.5 17.6 %copy-start.32 = (bf16[4,8,16,1,1152]{4,2,1,0,3:T(8,128)(2,1)S(1)}, bf16[4,8,16,1,1152]{4,2,1,0,3:T(8,128)(2,1)}, u32[]{:S(2)}) copy-start(bf16[4,8,16,1,1152]{4,2,1,0,3:T(8,128)(2,1)} %copy-done.31) | copy-start | bytes 3538948
  719.6 15.2 copy-start.4
  734.8 53.2 %copy-start.66 = (s32[1024]{0:T(1024)S(1)}, s32[1024]{0:T(1024)}, u32[]{:S(2)}) copy-start(s32[1024]{0:T(1024)} %get-tuple-element.87) | copy-start | bytes 12292
  787.9 46.4 %copy-start.67 = (f32[448]{0:T(512)S(1)}, f32[448]{0:T(512)}, u32[]{:S(2)}) copy-start(f32[448]{0:T(512)} %get-tuple-element.76) | copy-start | bytes 5380
  787.9 46.4 %copy-start.81 = (pred[448]{0:T(512)(128)(4,1)S(1)}, pred[448]{0:T(512)(128)(4,1)}, u32[]{:S(2)}) copy-start(pred[448]{0:T(512)(128)(4,1)} %get-tuple-element.75) | copy-start | bytes 1348
  911.5 726.7 %copy-start.47 = (f32[16128]{0:T(1024)S(1)}, f32[16128]{0:T(1024)}, u32[]{:S(2)}) copy-start(f32[16128]{0:T(1024)} %constant_dynamic-update-slice_fusion.10) | copy-start | bytes 193540
  911.5 769.4 %copy-start.33 = (f32[7,32,1152]{2,1,0:T(8,128)S(1)}, f32[7,32,1152]{2,1,0:T(8,128)}, u32[]{:S(2)}) copy-start(f32[7,32,1152]{2,1,0:T(8,128)} %param.32) | copy-start | bytes 3096580
  911.6 769.4 %copy-start.34 = (f32[7,32,1152]{2,1,0:T(8,128)S(1)}, f32[7,32,1152]{2,1,0:T(8,128)}, u32[]{:S(2)}) copy-start(f32[7,32,1152]{2,1,0:T(8,128)} %param.34) | copy-start | bytes 3096580
  911.6 769.4 %copy-start.78 = (f32[7]{0:T(128)S(1)}, f32[7]{0:T(128)}, u32[]{:S(2)}) copy-start(f32[7]{0:T(128)} %compare_convert_fusion) | copy-start | bytes 88
  1012.4 668.6 %copy-start.18 = (f32[7,32,1152]{2,1,0:T(8,128)S(1)}, f32[7,32,1152]{2,1,0:T(8,128)}, u32[]{:S(2)}) copy-start(f32[7,32,1152]{2,1,0:T(8,128)} %reduce-scatter.5.cloned.1.call-done) | copy-start | bytes 3096580
  1678.3 17.0 copy-start.40
  (65 other events, 329.0 us)
Sparse Core Ops, SparseCore 0:
  10.8 116.0 all-gather.2
  129.8 202.5 all-gather.4
  696.3 316.0 reduce-scatter.4
  1018.7 592.8 reduce-scatter.2
where the time goes:
time: 1720 us; the launch traced here: 1700 us
  waiting for transfers between devices  982 us (57%)
  local copies, waits for them, and re-layouts  225 us (13%)
  other arithmetic  210 us (12%)
  matrix products  187 us (11%)
  blocking collectives  64 us (4%)
    reduce_scatter x1, waiting for transfers between devices, on_device(): lax.psum_scatter(slot_rows(block_terms, tile_of_block), ('seq', 'batch'),...  597 us
    all_gather x1, waiting for transfers between devices, on_device(): lax.all_gather(block_low, ('seq', 'batch'), axis=0, tiled=True)  129 us
    all_gather x1, waiting for transfers between devices, on_device(): lax.all_gather(modulator_low, ('seq', 'batch'), axis=0, tiled=True)  114 us
    reduce_scatter x1, waiting for transfers between devices, on_device(): lax.psum_scatter(slot_rows(modul_terms, tile_of_modul), ('seq', 'batch'),...  101 us
    gather x2, local copies, waits for them, and re-layouts, slot_rows(): rows = jnp.take(terms, jnp.maximum(owners, 0), axis=0)  71.5 us
    mul x2, other arithmetic, slot_rows(): return rows * (owners >= 0).astype(jnp.float32)[:, None, None]  68 us
    concatenate x1, other arithmetic, on_device(): jnp.concatenate([grad_w_qkv, grad_w_out, grad_w_up, grad_w_down], axis=0)  53.2 us
    dot_general x5, matrix products, contract_last(): lax.dot_general(left, right, (((left.ndim - 1,), (1,)), ((), ())), prefer...  51.6 us
  transfers between devices with their start and end apart: 8, of which 8 were waited for; matrix products, arithmetic and copies ran while one was open for 17% of the time, Pallas kernels for 0%

commit v1 on v0

--- a/solution.py
+++ b/solution.py
@@ -13,6 +13,7 @@
 STEP = 5
 NT_W = 432
 NT_A = 216
+LANES = 128
 
 
 ln_eps = 1e-06
@@ -72,9 +73,16 @@
     return jax.vjp(function, values)[1](jnp.ones_like(values))[0]
 
 
-def slot_rows(terms, owners):
-    rows = jnp.take(terms, jnp.maximum(owners, 0), axis=0)
-    return rows * (owners >= 0).astype(jnp.float32)[:, None, None]
+def swap_everywhere(blocks):
+    return lax.all_to_all(blocks, ("seq", "batch"), split_axis=0, concat_axis=0, tiled=True)
+
+
+def sum_everywhere(terms, device_count):
+    rows = -(-terms.shape[0] // (device_count * LANES))
+    padded = jnp.pad(terms, (0, device_count * rows * LANES - terms.shape[0]))
+    mine = jnp.sum(swap_everywhere(padded.reshape(device_count, rows, LANES)), axis=0)
+    total = swap_everywhere(jnp.broadcast_to(mine, (device_count, rows, LANES)))
+    return total.reshape(-1)[: terms.shape[0]]
 
 
 def clip_factor(square_sum, count):
@@ -127,6 +135,8 @@
     seq_local = tokens.shape[0]
     frame_rows = tokens.shape[1]
     groups = lax.axis_size("seq")
+    batches = lax.axis_size("batch")
+    everywhere = ("seq", "batch")
     pair_local = frame_rows // groups
     device_count = lax.axis_size(("seq", "batch"))
     device_place = lax.axis_index(("seq", "batch"))
@@ -142,25 +152,45 @@
         .at[modulator_slots]
         .set(jnp.arange(NT_A, dtype=jnp.int32))
     )
-    gathered_block, gathered_modul = (
-        lax.all_gather(block_low, ("seq", "batch"), axis=0, tiled=True),
-        lax.all_gather(modulator_low, ("seq", "batch"), axis=0, tiled=True),
-    )
-    block_rows = jnp.take(gathered_block, block_slots, axis=0).reshape(NT_W * TR, D)
-    w_qkv = block_rows[: 3 * D]
-    w_out = block_rows[3 * D : 4 * D]
-    w_up = block_rows[4 * D : 4 * D + FF]
-    w_down = block_rows[4 * D + FF :]
-    w_modul = jnp.take(gathered_modul, modulator_slots, axis=0).reshape(6 * D, D)
+    gathered_block = lax.all_gather(block_low, everywhere, axis=0, tiled=True)
+
+    def weight_rows(first, count):
+        slots = block_slots[first // TR : (first + count) // TR]
+        tiles = gathered_block.at[slots].get(mode="promise_in_bounds")
+        return tiles.reshape(count, D)
+
+    w_qkv = weight_rows(0, 3 * D)
+    w_out = weight_rows(3 * D, D)
+    w_up = weight_rows(4 * D, FF)
+    w_down = weight_rows(4 * D + FF, FF)
     b_modul = biases[: 6 * D]
     b_query = biases[6 * D : 7 * D]
     b_value = biases[7 * D : 8 * D]
     b_out = biases[8 * D : 9 * D]
     b_up = biases[9 * D : 9 * D + FF]
     b_down = biases[9 * D + FF :]
+    own_rows = modul_local * TR
     cond_float = condition.astype(jnp.float32)
-    cond_low = swish(cond_float).astype(jnp.bfloat16)
-    modul = contract_last(cond_low, w_modul) + b_modul
+    cond_everyone = lax.all_to_all(
+        jnp.tile(condition, (batches, 1)), "batch", split_axis=0, concat_axis=0, tiled=True
+    )
+    cond_low = swish(cond_everyone.astype(jnp.float32)).astype(jnp.bfloat16)
+    modul_rows = modulator_low.reshape(own_rows, D)
+    modul_part = contract_last(cond_low, modul_rows).reshape(1, batches, seq_local, own_rows)
+    modul_slots = lax.all_to_all(
+        jnp.broadcast_to(modul_part, (groups, batches, seq_local, own_rows)).reshape(
+            device_count, seq_local, own_rows
+        ),
+        everywhere,
+        split_axis=0,
+        concat_axis=0,
+        tiled=True,
+    )
+    modul_slots = jnp.transpose(
+        modul_slots.reshape(device_count, seq_local, modul_local, TR), (0, 2, 1, 3)
+    ).reshape(device_count * modul_local, seq_local, TR)
+    modul = modul_slots.at[modulator_slots].get(mode="promise_in_bounds")
+    modul = jnp.transpose(modul, (1, 0, 2)).reshape(seq_local, 6 * D) + b_modul
     shift_one, scale_one, gate_one, shift_two, scale_two, gate_two = [
         piece[:, None, :] for piece in jnp.split(modul, 6, axis=1)
     ]
@@ -295,28 +325,65 @@
         axis=1,
     )
     cond_slope = slope_of(swish, cond_float)
-    w_modul_float = w_modul.astype(jnp.float32)
-    cond_low_float = cond_low.astype(jnp.float32)
-    cond_term = jnp.dot(d_modul, w_modul_float, precision=highest) * cond_slope
-    condition_grad = lax.psum(cond_term, "seq")
-    modul_terms = jnp.dot(d_modul.T, cond_low_float, precision=highest).reshape(NT_A, TR, D)
-    modulator_grad = lax.psum_scatter(
-        slot_rows(modul_terms, tile_of_modul), ("seq", "batch"), scatter_dimension=0, tiled=True
-    )
-    block_terms = jnp.concatenate([grad_w_qkv, grad_w_out, grad_w_up, grad_w_down], axis=0).reshape(
-        NT_W, TR, D
-    )
-    block_grad = lax.psum_scatter(
-        slot_rows(block_terms, tile_of_block), ("seq", "batch"), scatter_dimension=0, tiled=True
-    )
+    modul_owned = jnp.where(
+        (tile_of_modul >= 0)[:, None, None],
+        jnp.transpose(d_modul.reshape(seq_local, NT_A, TR), (1, 0, 2))
+        .at[jnp.maximum(tile_of_modul, 0)]
+        .get(mode="promise_in_bounds"),
+        0.0,
+    ).reshape(device_count, modul_local, seq_local, TR)
+    d_modul_mine = lax.all_to_all(
+        jnp.transpose(modul_owned, (0, 2, 1, 3)).reshape(device_count, seq_local, own_rows),
+        everywhere,
+        split_axis=0,
+        concat_axis=0,
+        tiled=True,
+    ).reshape(groups, batches * seq_local, own_rows)
+    d_modul_mine = jnp.sum(d_modul_mine, axis=0)
+    modulator_grad = lax.dot_general(
+        d_modul_mine,
+        cond_low.astype(jnp.float32),
+        (((0,), (0,)), ((), ())),
+        precision=highest,
+        preferred_element_type=jnp.float32,
+    ).reshape(modul_local, TR, D)
+    cond_terms = jnp.dot(d_modul_mine, modul_rows.astype(jnp.float32), precision=highest)
     bias_terms = jnp.concatenate(
         [jnp.sum(d_modul, axis=0), bias_query, bias_value, bias_out, bias_up, bias_down]
     )
-    bias_grad = lax.psum(bias_terms, ("seq", "batch"))
-    block_square, modul_square = lax.psum(
-        (jnp.sum(block_grad * block_grad), jnp.sum(modulator_grad * modulator_grad)),
-        ("seq", "batch"),
-    )
+    bias_count = bias_terms.shape[0]
+    small_sums = sum_everywhere(
+        jnp.concatenate(
+            [
+                bias_terms,
+                cond_terms.reshape(-1),
+                jnp.sum(modulator_grad * modulator_grad)[None],
+            ]
+        ),
+        device_count,
+    )
+    bias_grad = small_sums[:bias_count]
+    cond_sums = small_sums[bias_count : bias_count + cond_terms.size].reshape(cond_terms.shape)
+    modul_square = small_sums[bias_count + cond_terms.size]
+    condition_grad = cond_slope * lax.dynamic_slice_in_dim(
+        cond_sums, lax.axis_index("batch") * seq_local, seq_local
+    )
+    block_terms = jnp.concatenate(
+        [
+            grads.astype(jnp.bfloat16).reshape(-1, TR, D)
+            for grads in (grad_w_qkv, grad_w_out, grad_w_up, grad_w_down)
+        ]
+    )
+    block_owned = jnp.where(
+        (tile_of_block >= 0)[:, None, None],
+        block_terms.at[jnp.maximum(tile_of_block, 0)].get(mode="promise_in_bounds"),
+        0.0,
+    ).astype(jnp.bfloat16)
+    block_grad = lax.psum_scatter(
+        block_owned, everywhere, scatter_dimension=0, tiled=True
+    ).astype(jnp.float32)
+    square_terms = jnp.broadcast_to(jnp.sum(block_grad * block_grad), (device_count, 1, LANES))
+    block_square = jnp.sum(swap_everywhere(square_terms)[:, 0, 0])
     clip_block = clip_factor(block_square, float(NT_W * TR * D))
     clip_modul = clip_factor(modul_square, float(NT_A * TR * D))
     clip_bias = clip_factor(jnp.sum(bias_grad * bias_grad), float(bias_grad.shape[0]))

time: 1720 us -> 887 us (0.52)
  waiting for transfers between devices: 982 us -> 456 us
  other arithmetic: 210 us -> 89 us
  local copies, waits for them, and re-layouts: 225 us -> 138 us
  blocking collectives: 64 us -> 0 us
  matrix products: 187 us -> 140 us
  starting transfers between devices: 16.7 us -> 40.2 us
    reduce_scatter x2 -> x1, waiting for transfers between devices: 698 us -> 228 us  [on_device(): lax.psum_scatter(block_owned, everywhere, scatter_dimension=0, tiled=True)]
    all_gather x2 -> x1, waiting for transfers between devices: 242 us -> 143 us  [on_device(): gathered_block = lax.all_gather(block_low, everywhere, axis=0, tiled=True)]
    mul x2 -> x1, other arithmetic: 68 us -> 0.64 us  [on_device(): cond_slope * lax.dynamic_slice_in_dim(cond_sums, lax.axis_index('batch')...]
    psum x2 -> x0, blocking collectives: 64 us -> none  [the longest x1 40.1 us: on_device(): lax.psum((jnp.sum(block_grad * block_grad), jnp.sum(modulator_grad * modu...]
    gather x4 -> x7, local copies, waits for them, and re-layouts: 111 us -> 64 us  [the longest x4 37.1 us: weight_rows(): tiles = gathered_block.at[slots].get(mode='promise_in_bounds')]
    all_to_all x0 -> x6, waiting for transfers between devices: none -> 45.7 us  [the longest x3 27.2 us: swap_everywhere(): lax.all_to_all(blocks, ('seq', 'batch'), split_axis=0, concat_axis=0, til...]
    concatenate x1, other arithmetic: 53.2 us -> 21.6 us  [on_device(): jnp.concatenate([grads.astype(jnp.bfloat16).reshape(-1, TR, D) for grads...]
    dot_general x2, matrix products: 27.9 us -> 1.69 us  [the longest x1 1.34 us: on_device(): lax.dot_general(d_modul_mine, cond_low.astype(jnp.float32), (((0,), (0,))...]
  transfers between devices with their start and end apart: 8 -> 12, of which waited for: 8 -> 10; matrix products, arithmetic and copies ran while one was open for 17% -> 10% of each run, Pallas kernels for 0% -> 0%
where the time goes in v1:
time: 887 us; the launch traced here: 881 us
  waiting for transfers between devices  456 us (51%)
  matrix products  140 us (16%)
  local copies, waits for them, and re-layouts  138 us (16%)
  other arithmetic  89 us (10%)
  starting transfers between devices  40.2 us (5%)
  between operations  17.8 us (2%)
    reduce_scatter x1, waiting for transfers between devices, on_device(): lax.psum_scatter(block_owned, everywhere, scatter_dimension=0, tiled=True)  228 us
    all_gather x1, waiting for transfers between devices, on_device(): gathered_block = lax.all_gather(block_low, everywhere, axis=0, tiled=True)  143 us
    dot_general x4, matrix products, contract_first(): lax.dot_general(left, right, (((left.ndim - 1,), (0,)), ((), ())), prefer...  42.9 us
    dot_general x5, matrix products, contract_last(): lax.dot_general(left, right, (((left.ndim - 1,), (1,)), ((), ())), prefer...  41.7 us
    gather x4, local copies, waits for them, and re-layouts, weight_rows(): tiles = gathered_block.at[slots].get(mode='promise_in_bounds')  37.1 us
    dot_general x4, matrix products, token_outer(): lax.dot_general(grads, values, ((leading, leading), ((), ())), preferred_...  35.5 us
    all_to_all x3, waiting for transfers between devices, swap_everywhere(): lax.all_to_all(blocks, ('seq', 'batch'), split_axis=0, concat_axis=0, til...  27.2 us
    gather x1, local copies, waits for them, and re-layouts, on_device(): block_terms.at[jnp.maximum(tile_of_block, 0)].get(mode='promise_in_bounds')  24.9 us
  transfers between devices with their start and end apart: 12, of which 10 were waited for; matrix products, arithmetic and copies ran while one was open for 10% of the time, Pallas kernels for 0%

profile of v1, /device:TPU:0, one launch (start us, length us, event | category | flops | bytes accessed | tf_op | source)
XLA Modules:
  0.0 881.2 jit_solution(10259218573718562557)
XLA Ops:
  9.3 6.3 all-to-all-start
  23.0 6.1 all-to-all-start.1
  29.1 10.2 %all-to-all-done.1 = f32[32,4,224]{2,1,0:T(4,128)S(1)} async-done(((f32[32,4,224]{2,1,0:T(4,128)}), f32[32,4,224]{2,1,0:T(4,128)S(1)}, u32[]{:S(2)}, u32[]{:S(2)}) %all-to-all-start.1) | async-done | bytes 114720 | tf_op jit(solution)/shard_map/all_to_all | solution.py:180
  47.7 21.6 %all-to-all-done.2 = bf16[4,16,8,1152]{3,1,0,2:T(8,128)(2,1)S(1)} async-done(((bf16[4,16,8,1152]{3,1,0,2:T(8,128)(2,1)}), bf16[4,16,8,1152]{3,1,0,2:T(8,128)(2,1)S(1)}, u32[]{:S(2)}, u32[]{:S(2)}) %all-to-all-start.2) | async-done | bytes 1179680 | tf_op jit(solution)/shard_map/all_to_all | solution.py:200
  70.4 142.9 %all-gather.2.cloned.1.call-done = bf16[448,32,1152]{2,1,0:T(8,128)(2,1)} async-done(((bf16[14,32,1152]{2,1,0:T(8,128)(2,1)}), bf16[448,32,1152]{2,1,0:T(8,128)(2,1)}) %all-gather.2.cloned.1.call-update) | async-done | bytes 33030160 | tf_op jit(solution)/shard_map/all_gather | solution.py:155
  213.3 8.8 gather_fusion.1
  222.1 8.5 add_convert_fusion
  232.5 5.7 reshape.276
  238.2 5.7 reshape.277
  279.0 12.0 %gather_fusion.4 = bf16[144,32,1152]{2,1,0:T(8,128)(2,1)} fusion(bf16[448,32,1152]{2,1,0:T(8,128)(2,1)} %all-gather.2.cloned.1.call-done, s32[1024]{0:T(1024)S(1)} %get-tuple-element.85), kind=kCustom, calls=%fused_computation.4 | custom fusion | bytes 21234240 | tf_op jit(solution)/shard_map/gather | solution.py:159
  291.0 12.1 %gather_fusion.3 = bf16[144,32,1152]{2,1,0:T(8,128)(2,1)} fusion(bf16[448,32,1152]{2,1,0:T(8,128)(2,1)} %all-gather.2.cloned.1.call-done, s32[1024]{0:T(1024)S(1)} %get-tuple-element.86), kind=kCustom, calls=%fused_computation.3 | custom fusion | bytes 21234240 | tf_op jit(solution)/shard_map/gather | solution.py:159
  305.5 13.4 %fusion.76 = f32[4,128,4608]{2,1,0:T(8,128)} fusion(bf16[4608,1152,1]{1,0,2:T(8,128)(2,1)} %bitcast.169, f32[4,128,1152]{2,1,0:T(8,128)S(1)} %get-tuple-element.45, f32[4,1152]{1,0:T(4,128)S(1)} %get-tuple-element.63, f32[4,1152]{1,0:T(4,128)S(1)} %get-tuple-element.64, f32[4,128]{1,0:T(4,128)S(1)} %add_rsqrt_fusion, f32[4,128]{1,0:T(4,128)S(1)} %broadcast_multiply_fusion.9), kind=kOutput, calls=%fused_computation.172 | convolution fusion | flops 5438767104 | bytes 22454272 | tf_op jit(solution)/shard_map/dot_general | solution.py:32
  318.9 13.4 %fusion.2 = bf16[4608,1152]{1,0:T(8,128)(2,1)} fusion(bf16[4,128,1152]{2,1,0:T(8,128)(2,1)S(1)} %copy-done.59, f32[4,1152]{1,0:T(4,128)S(1)} %get-tuple-element.62, f32[4,128,4608]{2,1,0:T(8,128)} %fusion.76, f32[4608]{0:T(1024)S(1)} %slice.81), kind=kOutput, calls=%fused_computation.15 | convolution fusion | flops 5466488832 | bytes 21270528 | tf_op jit(solution)/shard_map/dot_general | solution.py:45
  332.4 15.9 %convert_reduce_fusion = (f32[4608]{0:T(1024)}, bf16[4,128,4608]{2,1,0:T(8,128)(2,1)}) fusion(f32[4,128,4608]{2,1,0:T(8,128)} %fusion.76, f32[4608]{0:T(1024)S(1)} %slice.81, bf16[4608,1152,1]{1,0,2:T(8,128)(2,1)S(1)} %bitcast.167, bf16[4,128,1152]{2,1,0:T(8,128)(2,1)} %param.23, f32[4,1152]{1,0:T(4,128)S(1)} %get-tuple-element.62), kind=kOutput, calls=%fused_computation.28 | convolution fusion | flops 5489487360 | bytes 26007552 | tf_op jit(solution)/shard_map/dot_general | solution.py:32
  348.3 13.3 %multiply_reduce_fusion.1 = (f32[4,1152]{1,0:T(4,128)}, f32[4,128]{1,0:T(4,128)S(1)}, f32[4,128]{1,0:T(4,128)S(1)}, f32[4,1152]{1,0:T(4,128)}, f32[4,128,1152]{2,1,0:T(8,128)}) fusion(f32[4,128,1152]{2,1,0:T(8,128)S(1)} %copy-done.9, f32[4,128]{1,0:T(4,128)S(1)} %add_rsqrt_fusion, f32[4,128]{1,0:T(4,128)S(1)} %broadcast_multiply_fusion.9, ...), kind=kOutput, calls=%fused_computation.83 | convolution fusion | flops 5441116160 | bytes 20117504 | tf_op jit(solution)/shard_map/dot_general | solution.py:38
  361.6 14.5 %convert_reduce_fusion.2 = (f32[1152]{0:T(1024)}, f32[4,1152]{1,0:T(4,128)}, bf16[4,128,1152]{2,1,0:T(8,128)(2,1)}, f32[4,1152]{1,0:T(4,128)}, f32[4,128,1152]{2,1,0:T(8,128)}) fusion(bf16[4,128,1152]{2,1,0:T(8,128)(2,1)} %param.23, f32[4,1152]{1,0:T(4,128)S(1)} %get-tuple-element.62, f32[4,128,1152]{2,1,0:T(8,128)S(1)} %copy-done.9, ...), kind=kOutput, calls=%fused_computation.81 | convolution fusion | flops 5471787008 | bytes 31960064 | tf_op jit(solution)/shard_map/dot_general | solution.py:38
  383.3 11.7 %fusion.1 = bf16[4608,1152]{1,0:T(8,128)(2,1)} fusion(bf16[4,128,4608]{2,1,0:T(8,128)(2,1)} %get-tuple-element.80, f32[4,128,1152]{2,1,0:T(8,128)} %copy-done.8, f32[4,1152]{1,0:T(4,128)S(1)} %get-tuple-element.63, f32[4,1152]{1,0:T(4,128)S(1)} %get-tuple-element.64, f32[4,128]{1,0:T(4,128)S(1)} %add_rsqrt_fusion, f32[4,128]{1,0:T(4,128)S(1)} %broadcast_multiply_fusion.9), kind=kOutput, calls=%fused_computation.14 | convolution fusion | flops 5444075520 | bytes 17735680 | tf_op jit(solution)/shard_map/dot_general | solution.py:45
  395.0 5.0 all-to-all-done.4
  408.4 5.0 reshape.284
  449.2 7.1 fusion.3
  456.3 21.6 %pad_maximum_fusion = bf16[432,32,1152]{2,1,0:T(8,128)(2,1)} fusion(bf16[144,32,1152]{2,1,0:T(8,128)(2,1)} %bitcast.171, bf16[144,32,1152]{2,1,0:T(8,128)(2,1)} %bitcast.172, bf16[36,32,1152]{2,1,0:T(8,128)(2,1)S(1)} %bitcast.179, bf16[108,32,1152]{2,1,0:T(8,128)(2,1)} %bitcast.175), kind=kLoop, calls=%fused_computation.11 | loop fusion | flops 47775744 | bytes 63700992 | tf_op jit(solution)/shard_map/concatenate | solution.py:371
  477.9 24.9 %gather_fusion.6 = bf16[448,32,1152]{2,1,0:T(8,128)(2,1)} fusion(bf16[432,32,1152]{2,1,0:T(8,128)(2,1)} %pad_maximum_fusion, s32[1024]{0:T(1024)S(1)} %copy-done.52), kind=kCustom, calls=%fused_computation.6 | custom fusion | bytes 66062080 | tf_op jit(solution)/shard_map/gather | solution.py:379
  502.9 22.6 %broadcast_select_fusion = bf16[448,32,1152]{2,1,0:T(8,128)(2,1)} fusion(bf16[448,32,1152]{2,1,0:T(8,128)(2,1)} %gather_fusion.6, pred[448]{0:T(512)(128)(4,1)S(1)} %copy-done.55), kind=kLoop, calls=%fused_computation.10 | loop fusion | flops 16515072 | bytes 66060736 | tf_op jit(solution)/shard_map/jit(_where)/select_n | solution.py:377
  526.3 10.1 %fusion.21 = bf16[4,128,1,1152]{3,1,0,2:T(8,128)(2,1)S(1)} fusion(bf16[4,16,8,3456]{3,2,1,0:T(8,128)(2,1)} %copy-done.12, bf16[3456,1152,1,1]{1,0,3,2:T(8,128)(2,1)} %bitcast.174), kind=kOutput, calls=%fused_computation.62 | convolution fusion | flops 4077453312 | bytes 12681216 | tf_op jit(solution)/shard_map/dot_general | solution.py:38
  546.6 12.2 %all-to-all-done.5 = bf16[4,128,1,1152]{3,0,2,1:T(4,128)(2,1)S(1)} async-done(((bf16[4,128,1,1152]{3,0,2,1:T(4,128)(2,1)}), bf16[4,128,1,1152]{3,0,2,1:T(4,128)(2,1)S(1)}, u32[]{:S(2)}, u32[]{:S(2)}) %all-to-all-start.5) | async-done | bytes 1179680 | tf_op jit(solution)/shard_map/all_to_all | solution.py:303
  566.5 8.3 all-to-all-done.6
  580.9 10.0 %all-to-all-done.7 = f32[32,9,128]{2,1,0:T(8,128)S(1)} async-done(((f32[32,9,128]{2,1,0:T(8,128)}), f32[32,9,128]{2,1,0:T(8,128)S(1)}, u32[]{:S(2)}, u32[]{:S(2)}) %all-to-all-start.7) | async-done | bytes 147488 | tf_op jit(solution)/shard_map/all_to_all | solution.py:77
  594.4 5.1 fusion.28
  599.4 10.6 %all-to-all-done.8 = f32[32,9,128]{2,1,0:T(8,128)S(1)} async-done(((f32[32,9,128]{2,1,0:T(8,128)}), f32[32,9,128]{2,1,0:T(8,128)S(1)}, u32[]{:S(2)}, u32[]{:S(2)}) %all-to-all-start.8) | async-done | bytes 147488 | tf_op jit(solution)/shard_map/all_to_all | solution.py:77
  619.6 227.6 %reduce-scatter.2.cloned.1.call-done = bf16[14,32,1152]{2,1,0:T(8,128)(2,1)} async-done(((bf16[448,32,1152]{2,1,0:T(8,128)(2,1)}), bf16[14,32,1152]{2,1,0:T(8,128)(2,1)}) %reduce-scatter.2.cloned.1.call-update) | async-done | bytes 1032208 | tf_op jit(solution)/shard_map/reduce_scatter | solution.py:382
  855.8 6.5 all-to-all-done.9
  863.7 8.7 fusion.87
  (284 shorter events, 155.8 us)
Async XLA Ops:
  7.2 14.8 %copy-start = (bf16[7,32,1152]{2,1,0:T(8,128)(2,1)S(1)}, bf16[7,32,1152]{2,1,0:T(8,128)(2,1)}, u32[]{:S(2)}) copy-start(bf16[7,32,1152]{2,1,0:T(8,128)(2,1)} %param.31) | copy-start | bytes 1548292
  7.2 206.1 %all-gather.2.cloned.1.call-start = ((), (), s32[]{:S(2)}) async-start(), calls=%async_computation.11 | async-start | bytes 34062336 | tf_op jit(solution)/shard_map/all_gather | solution.py:155
  9.3 12.6 %all-to-all-start = ((bf16[4,4,1152]{2,1,0:T(4,128)(2,1)}), bf16[4,4,1152]{2,1,0:T(4,128)(2,1)S(1)}, u32[]{:S(2)}, u32[]{:S(2)}) async-start(bf16[4,4,1152]{2,1,0:T(4,128)(2,1)} %tile.2), calls=%async_computation | async-start | bytes 73728 | tf_op jit(solution)/shard_map/all_to_all | solution.py:174
  16.9 24.1 %copy-start.41 = (f32[4,128]{1,0:T(4,128)}, f32[4,128]{1,0:T(4,128)S(1)}, u32[]{:S(2)}) copy-start(f32[4,128]{1,0:T(4,128)S(1)} %broadcast_multiply_fusion.10) | copy-start | bytes 6148
  19.0 258.7 %copy-start.57 = (s32[224]{0:T(256)}, s32[224]{0:T(256)S(1)}, u32[]{:S(2)}) copy-start(s32[224]{0:T(256)S(1)} %scatter_custom_fusion) | copy-start | bytes 2692
  21.9 256.5 %copy-start.47 = (s32[448]{0:T(512)}, s32[448]{0:T(512)S(1)}, u32[]{:S(2)}) copy-start(s32[448]{0:T(512)S(1)} %scatter_custom_fusion.1) | copy-start | bytes 5380
  22.3 18.7 %slice-start.3 = ((f32[16128]{0:T(1024)}), f32[6912]{0:T(1024)S(1)}, s32[]{:S(2)}) async-start(f32[16128]{0:T(1024)} %param.36), calls=%async_computation.16 | async-start | bytes 57344 | tf_op jit(solution)/shard_map/slice | solution.py:166
  23.0 16.3 %all-to-all-start.1 = ((f32[32,4,224]{2,1,0:T(4,128)}), f32[32,4,224]{2,1,0:T(4,128)S(1)}, u32[]{:S(2)}, u32[]{:S(2)}) async-start(f32[32,4,224]{2,1,0:T(4,128)} %bitcast.2), calls=%async_computation.1 | async-start | bytes 262144 | tf_op jit(solution)/shard_map/all_to_all | solution.py:180
  43.7 25.6 %all-to-all-start.2 = ((bf16[4,16,8,1152]{3,1,0,2:T(8,128)(2,1)}), bf16[4,16,8,1152]{3,1,0,2:T(8,128)(2,1)S(1)}, u32[]{:S(2)}, u32[]{:S(2)}) async-start(bf16[4,16,8,1152]{3,1,0,2:T(8,128)(2,1)} %copy.162), calls=%async_computation.2 | async-start | bytes 2359296 | tf_op jit(solution)/shard_map/all_to_all | solution.py:200
  273.7 29.4 %all-to-all-start.3 = ((bf16[4,128,1,1152]{3,0,2,1:T(4,128)(2,1)}), bf16[4,128,1,1152]{3,0,2,1:T(4,128)(2,1)S(1)}, u32[]{:S(2)}, u32[]{:S(2)}) async-start(bf16[4,128,1,1152]{3,0,2,1:T(4,128)(2,1)} %copy.170), calls=%async_computation.3 | async-start | bytes 2359296 | tf_op jit(solution)/shard_map/all_to_all | solution.py:235
  305.1 13.8 %copy-start.8 = (f32[4,128,1152]{2,1,0:T(8,128)}, f32[4,128,1152]{2,1,0:T(8,128)S(1)}, u32[]{:S(2)}) copy-start(f32[4,128,1152]{2,1,0:T(8,128)S(1)} %get-tuple-element.45) | copy-start | bytes 7077892
  305.5 13.4 %copy-start.59 = (bf16[4,128,1152]{2,1,0:T(8,128)(2,1)S(1)}, bf16[4,128,1152]{2,1,0:T(8,128)(2,1)}, u32[]{:S(2)}) copy-start(bf16[4,128,1152]{2,1,0:T(8,128)(2,1)} %param.23) | copy-start | bytes 3538948
  305.5 26.9 %slice-start = ((s8[10616832]{0:T(1024)(128)(4,1)}), s8[4194304]{0:T(1024)(128)(4,1)S(1)}, s32[]{:S(2)}) async-start(s8[10616832]{0:T(1024)(128)(4,1)} %bitcast.165), calls=%async_computation.13 | async-start | bytes 8388608
  305.5 26.8 %slice-start.1 = ((s8[10616832]{0:T(1024)(128)(4,1)}), s8[4194304]{0:T(1024)(128)(4,1)S(1)}, s32[]{:S(2)}) async-start(s8[10616832]{0:T(1024)(128)(4,1)} %bitcast.165), calls=%async_computation.14 | async-start | bytes 8388608
  318.9 13.5 %slice-start.2 = ((s8[10616832]{0:T(1024)(128)(4,1)}), s8[2228224]{0:T(1024)(128)(4,1)S(1)}, s32[]{:S(2)}) async-start(s8[10616832]{0:T(1024)(128)(4,1)} %bitcast.165), calls=%async_computation.15 | async-start | bytes 4456448
  332.3 15.9 %copy-start.9 = (f32[4,128,1152]{2,1,0:T(8,128)S(1)}, f32[4,128,1152]{2,1,0:T(8,128)}, u32[]{:S(2)}) copy-start(f32[4,128,1152]{2,1,0:T(8,128)} %copy-done.8) | copy-start | bytes 7077892
  379.0 20.9 %all-to-all-start.4 = ((bf16[4,16,8,1152]{3,1,0,2:T(8,128)(2,1)}), bf16[4,16,8,1152]{3,1,0,2:T(8,128)(2,1)S(1)}, u32[]{:S(2)}, u32[]{:S(2)}) async-start(bf16[4,16,8,1152]{3,1,0,2:T(8,128)(2,1)} %copy.172), calls=%async_computation.4 | async-start | bytes 2359296 | tf_op jit(solution)/shard_map/all_to_all | solution.py:265
  383.2 464.0 %reduce-scatter.2.cloned.1.call-start = ((), (), s32[]{:S(2)}) async-start(), calls=%async_computation.12 | async-start | bytes 34062336 | tf_op jit(solution)/shard_map/reduce_scatter | solution.py:382
  456.3 21.6 %copy-start.52 = (s32[1024]{0:T(1024)S(1)}, s32[1024]{0:T(1024)}, u32[]{:S(2)}) copy-start(s32[1024]{0:T(1024)} %get-tuple-element.83) | copy-start | bytes 12292
  477.9 25.0 %copy-start.55 = (pred[448]{0:T(512)(128)(4,1)S(1)}, pred[448]{0:T(512)(128)(4,1)}, u32[]{:S(2)}) copy-start(pred[448]{0:T(512)(128)(4,1)} %broadcast_compare_fusion.1) | copy-start | bytes 1348
  538.3 20.5 %all-to-all-start.5 = ((bf16[4,128,1,1152]{3,0,2,1:T(4,128)(2,1)}), bf16[4,128,1,1152]{3,0,2,1:T(4,128)(2,1)S(1)}, u32[]{:S(2)}, u32[]{:S(2)}) async-start(bf16[4,128,1,1152]{3,0,2,1:T(4,128)(2,1)} %copy.183), calls=%async_computation.5 | async-start | bytes 2359296 | tf_op jit(solution)/shard_map/all_to_all | solution.py:303
  563.8 11.0 %all-to-all-start.6 = ((f32[32,4,224]{2,1,0:T(4,128)}), f32[32,4,224]{2,1,0:T(4,128)S(1)}, u32[]{:S(2)}, u32[]{:S(2)}) async-start(f32[32,4,224]{2,1,0:T(4,128)} %reshape.397), calls=%async_computation.6 | async-start | bytes 262144 | tf_op jit(solution)/shard_map/all_to_all | solution.py:335
  578.1 12.8 %all-to-all-start.7 = ((f32[32,9,128]{2,1,0:T(8,128)}), f32[32,9,128]{2,1,0:T(8,128)S(1)}, u32[]{:S(2)}, u32[]{:S(2)}) async-start(f32[32,9,128]{2,1,0:T(8,128)} %reshape.293), calls=%async_computation.7 | async-start | bytes 524288 | tf_op jit(solution)/shard_map/all_to_all | solution.py:77
  591.7 18.4 %all-to-all-start.8 = ((f32[32,9,128]{2,1,0:T(8,128)}), f32[32,9,128]{2,1,0:T(8,128)S(1)}, u32[]{:S(2)}, u32[]{:S(2)}) async-start(f32[32,9,128]{2,1,0:T(8,128)} %broadcast_in_dim.130), calls=%async_computation.8 | async-start | bytes 524288 | tf_op jit(solution)/shard_map/all_to_all | solution.py:77
  594.3 18.4 %copy-start.32 = (f32[16128]{0:T(1024)S(1)}, f32[16128]{0:T(1024)}, u32[]{:S(2)}) copy-start(f32[16128]{0:T(1024)} %param.36) | copy-start | bytes 193540
  594.3 18.4 %copy-start.38 = (f32[16128]{0:T(1024)S(1)}, f32[16128]{0:T(1024)}, u32[]{:S(2)}) copy-start(f32[16128]{0:T(1024)} %param.39) | copy-start | bytes 193540
  594.3 18.4 %copy-start.39 = (f32[16128]{0:T(1024)S(1)}, f32[16128]{0:T(1024)}, u32[]{:S(2)}) copy-start(f32[16128]{0:T(1024)} %param.37) | copy-start | bytes 193540
  594.3 18.4 %copy-start.40 = (f32[16128]{0:T(1024)S(1)}, f32[16128]{0:T(1024)}, u32[]{:S(2)}) copy-start(f32[16128]{0:T(1024)} %param.38) | copy-start | bytes 193540
  599.4 14.0 %copy-start.26 = (f32[7,32,1152]{2,1,0:T(8,128)S(1)}, f32[7,32,1152]{2,1,0:T(8,128)}, u32[]{:S(2)}) copy-start(f32[7,32,1152]{2,1,0:T(8,128)} %param.32) | copy-start | bytes 3096580
  618.4 236.7 %copy-start.43 = (bf16[4,1152]{1,0:T(4,128)(2,1)S(1)}, bf16[4,1152]{1,0:T(4,128)(2,1)}, u32[]{:S(2)}) copy-start(bf16[4,1152]{1,0:T(4,128)(2,1)} %param.21) | copy-start | bytes 27652
  618.4 245.2 %copy-start.20 = (f32[14,32,1152]{2,1,0:T(8,128)S(1)}, f32[14,32,1152]{2,1,0:T(8,128)}, u32[]{:S(2)}) copy-start(f32[14,32,1152]{2,1,0:T(8,128)} %param.27) | copy-start | bytes 6193156
  850.9 11.4 %all-to-all-start.9 = ((f32[32,1,128]{2,1,0:T(1,128)}), f32[32,1,128]{2,1,0:T(1,128)S(1)}, u32[]{:S(2)}, u32[]{:S(2)}) async-start(f32[32,1,128]{2,1,0:T(1,128)} %broadcast_in_dim.136), calls=%async_computation.10 | async-start | bytes 32768 | tf_op jit(solution)/shard_map/all_to_all | solution.py:77
  (44 other events, 249.8 us)
Sparse Core Ops, SparseCore 0:
  10.9 202.3 all-gather.1
  525.6 321.5 reduce-scatter.1

commit v2 on v1

--- a/solution.py
+++ b/solution.py
@@ -83,6 +83,27 @@
     mine = jnp.sum(swap_everywhere(padded.reshape(device_count, rows, LANES)), axis=0)
     total = swap_everywhere(jnp.broadcast_to(mine, (device_count, rows, LANES)))
     return total.reshape(-1)[: terms.shape[0]]
+
+
+def halve_to_owner(terms, far_first):
+    groups, batches = terms.shape[:2]
+    seq_bits, batch_bits = groups.bit_length() - 1, batches.bit_length() - 1
+    rest = list(range(1, seq_bits))
+    order = [0] + (rest[::-1] if far_first else rest)
+    steps = [("seq", bit) for bit in order] + [("batch", bit) for bit in range(batch_bits)]
+    left = [("seq", bit) for bit in reversed(range(seq_bits))]
+    left += [("batch", bit) for bit in reversed(range(batch_bits))]
+    terms = terms.reshape((2,) * len(left) + terms.shape[2:])
+    for axis, bit in steps:
+        dim = left.index((axis, bit))
+        left.pop(dim)
+        side = (lax.axis_index(axis) >> bit) & 1
+        sent = lax.dynamic_index_in_dim(terms, 1 - side, dim, keepdims=False)
+        kept = lax.dynamic_index_in_dim(terms, side, dim, keepdims=False)
+        pairs = [(place, place ^ (1 << bit)) for place in range(lax.axis_size(axis))]
+        arrived = lax.ppermute(sent.astype(jnp.bfloat16), axis, pairs)
+        terms = kept.astype(jnp.float32) + arrived.astype(jnp.float32)
+    return terms
 
 
 def clip_factor(square_sum, count):
@@ -374,20 +395,27 @@
             for grads in (grad_w_qkv, grad_w_out, grad_w_up, grad_w_down)
         ]
     )
-    block_owned = jnp.where(
-        (tile_of_block >= 0)[:, None, None],
-        block_terms.at[jnp.maximum(tile_of_block, 0)].get(mode="promise_in_bounds"),
-        0.0,
-    ).astype(jnp.bfloat16)
-    block_grad = lax.psum_scatter(
-        block_owned, everywhere, scatter_dimension=0, tiled=True
-    ).astype(jnp.float32)
+    block_mine = lax.dynamic_slice_in_dim(tile_of_block, device_place * block_local, block_local)
+    half_terms = block_terms.reshape(NT_W * 2, TR // 2, D)
+    owner_tiles = jnp.maximum(tile_of_block, 0).reshape(device_count, block_local)
+    chunk = block_local // 2 if block_local % 2 == 0 else block_local
+    pieces = []
+    for start in range(0, block_local, chunk):
+        tiles = owner_tiles[:, start : start + chunk].reshape(-1)
+        halves = []
+        for half in range(2):
+            owned = half_terms.at[tiles * 2 + half].get(mode="promise_in_bounds")
+            owned = owned.reshape(groups, batches, chunk, TR // 2, D)
+            halves.append(halve_to_owner(owned, half == 1))
+        pieces.append(jnp.concatenate(halves, axis=1))
+    block_grad = jnp.where(
+        (block_mine >= 0)[:, None, None], jnp.concatenate(pieces, axis=0), 0.0
+    )
     square_terms = jnp.broadcast_to(jnp.sum(block_grad * block_grad), (device_count, 1, LANES))
     block_square = jnp.sum(swap_everywhere(square_terms)[:, 0, 0])
     clip_block = clip_factor(block_square, float(NT_W * TR * D))
     clip_modul = clip_factor(modul_square, float(NT_A * TR * D))
     clip_bias = clip_factor(jnp.sum(bias_grad * bias_grad), float(bias_grad.shape[0]))
-    block_mine = lax.dynamic_slice_in_dim(tile_of_block, device_place * block_local, block_local)
     block_live = (block_mine >= 0).astype(jnp.float32)[:, None, None]
     modul_mine = lax.dynamic_slice_in_dim(tile_of_modul, device_place * modul_local, modul_local)
     modul_live = (modul_mine >= 0).astype(jnp.float32)[:, None, None]

time: 887 us -> 886 us (level)
  waiting for transfers between devices: 456 us -> 356 us
  local copies, waits for them, and re-layouts: 138 us -> 203 us
  other arithmetic: 89 us -> 105 us
  starting transfers between devices: 40.2 us -> 56.2 us
    reduce_scatter x1 -> x0, waiting for transfers between devices: 228 us -> none  [on_device(): lax.psum_scatter(block_owned, everywhere, scatter_dimension=0, tiled=True)]
    ppermute x0 -> x20, waiting for transfers between devices: none -> 147 us  [halve_to_owner(): arrived = lax.ppermute(sent.astype(jnp.bfloat16), axis, pairs)]
    add x0 -> x20, other arithmetic: none -> 33.4 us  [halve_to_owner(): terms = kept.astype(jnp.float32) + arrived.astype(jnp.float32)]
    dynamic_slice x0 -> x6, local copies, waits for them, and re-layouts: none -> 29.2 us  [the longest x3 19.8 us: halve_to_owner(): kept = lax.dynamic_index_in_dim(terms, side, dim, keepdims=False)]
    select_n x1, other arithmetic: 22.6 us -> 0.01 us  [on_device(): owned = half_terms.at[tiles * 2 + half].get(mode='promise_in_bounds')]
    gather x1 -> x4, local copies, waits for them, and re-layouts: 24.9 us -> 43.9 us  [on_device(): owned = half_terms.at[tiles * 2 + half].get(mode='promise_in_bounds')]
    ppermute x0 -> x20, starting transfers between devices: none -> 15.5 us  [halve_to_owner(): arrived = lax.ppermute(sent.astype(jnp.bfloat16), axis, pairs)]
    all_to_all x1, waiting for transfers between devices: 12.2 us -> 0.01 us  [on_device(): lax.all_to_all(d_act_one.reshape(seq_local, frame_rows, 1, D), 'seq', spl...]
  transfers between devices with their start and end apart: 12 -> 31, of which waited for: 10 -> 19; matrix products, arithmetic and copies ran while one was open for 10% -> 25% of each run, Pallas kernels for 0% -> 0%
where the time goes in v2:
time: 886 us; the launch traced here: 878 us
  waiting for transfers between devices  356 us (40%)
  local copies, waits for them, and re-layouts  203 us (23%)
  matrix products  140 us (16%)
  other arithmetic  105 us (12%)
  starting transfers between devices  56.2 us (6%)
  between operations  18.1 us (2%)
    ppermute x20, waiting for transfers between devices, halve_to_owner(): arrived = lax.ppermute(sent.astype(jnp.bfloat16), axis, pairs)  147 us
    all_gather x1, waiting for transfers between devices, on_device(): gathered_block = lax.all_gather(block_low, everywhere, axis=0, tiled=True)  141 us
    gather x4, local copies, waits for them, and re-layouts, on_device(): owned = half_terms.at[tiles * 2 + half].get(mode='promise_in_bounds')  43.9 us
    dot_general x4, matrix products, contract_first(): lax.dot_general(left, right, (((left.ndim - 1,), (0,)), ((), ())), prefer...  42.4 us
    dot_general x5, matrix products, contract_last(): lax.dot_general(left, right, (((left.ndim - 1,), (1,)), ((), ())), prefer...  41.6 us
    gather x4, local copies, waits for them, and re-layouts, weight_rows(): tiles = gathered_block.at[slots].get(mode='promise_in_bounds')  36.1 us
    dot_general x4, matrix products, token_outer(): lax.dot_general(grads, values, ((leading, leading), ((), ())), preferred_...  35.5 us
    add x20, other arithmetic, halve_to_owner(): terms = kept.astype(jnp.float32) + arrived.astype(jnp.float32)  33.4 us
  transfers between devices with their start and end apart: 31, of which 19 were waited for; matrix products, arithmetic and copies ran while one was open for 25% of the time, Pallas kernels for 0%

profile of v2, /device:TPU:0, one launch (start us, length us, event | category | flops | bytes accessed | tf_op | source)
XLA Modules:
  0.0 878.3 jit_solution(14018402176079956279)
XLA Ops:
  31.7 10.2 %all-to-all-done.1 = f32[32,4,224]{2,1,0:T(4,128)S(1)} async-done(((f32[32,4,224]{2,1,0:T(4,128)}), f32[32,4,224]{2,1,0:T(4,128)S(1)}, u32[]{:S(2)}, u32[]{:S(2)}) %all-to-all-start.1) | async-done | bytes 114720 | tf_op jit(solution)/shard_map/all_to_all | solution.py:201
  51.2 22.3 %all-to-all-done.2 = bf16[4,16,8,1152]{3,1,0,2:T(8,128)(2,1)S(1)} async-done(((bf16[4,16,8,1152]{3,1,0,2:T(8,128)(2,1)}), bf16[4,16,8,1152]{3,1,0,2:T(8,128)(2,1)S(1)}, u32[]{:S(2)}, u32[]{:S(2)}) %all-to-all-start.2) | async-done | bytes 1179680 | tf_op jit(solution)/shard_map/all_to_all | solution.py:221
  74.6 140.6 %all-gather.2.cloned.1.call-done = bf16[448,32,1152]{2,1,0:T(8,128)(2,1)} async-done(((bf16[14,32,1152]{2,1,0:T(8,128)(2,1)}), bf16[448,32,1152]{2,1,0:T(8,128)(2,1)}) %all-gather.2.cloned.1.call-update) | async-done | bytes 33030160 | tf_op jit(solution)/shard_map/all_gather | solution.py:176
  215.1 8.6 gather_fusion.1
  223.7 8.5 add_convert_fusion
  282.6 11.7 %gather_fusion.4 = bf16[144,32,1152]{2,1,0:T(8,128)(2,1)} fusion(bf16[448,32,1152]{2,1,0:T(8,128)(2,1)} %all-gather.2.cloned.1.call-done, s32[1024]{0:T(1024)S(1)} %get-tuple-element.100), kind=kCustom, calls=%fused_computation.4 | custom fusion | bytes 21234240 | tf_op jit(solution)/shard_map/gather | solution.py:180
  294.3 11.7 %gather_fusion.3 = bf16[144,32,1152]{2,1,0:T(8,128)(2,1)} fusion(bf16[448,32,1152]{2,1,0:T(8,128)(2,1)} %all-gather.2.cloned.1.call-done, s32[1024]{0:T(1024)S(1)} %get-tuple-element.101), kind=kCustom, calls=%fused_computation.3 | custom fusion | bytes 21234240 | tf_op jit(solution)/shard_map/gather | solution.py:180
  308.4 13.3 %fusion.89 = f32[4,128,4608]{2,1,0:T(8,128)} fusion(bf16[4608,1152,1]{1,0,2:T(8,128)(2,1)} %bitcast.288, f32[4,128,1152]{2,1,0:T(8,128)S(1)} %get-tuple-element.47, f32[4,1152]{1,0:T(4,128)S(1)} %get-tuple-element.72, f32[4,1152]{1,0:T(4,128)S(1)} %get-tuple-element.73, f32[4,128]{1,0:T(4,128)S(1)} %add_rsqrt_fusion, ...), kind=kOutput, calls=%fused_computation.241 | convolution fusion | flops 5438767104 | bytes 22454272 | tf_op jit(solution)/shard_map/dot_general | solution.py:32
  321.7 13.3 %fusion.2 = bf16[4608,1152]{1,0:T(8,128)(2,1)} fusion(bf16[4,128,1152]{2,1,0:T(8,128)(2,1)S(1)} %copy-done.61, f32[4,1152]{1,0:T(4,128)S(1)} %get-tuple-element.71, f32[4,128,4608]{2,1,0:T(8,128)} %fusion.89, f32[4608]{0:T(1024)S(1)} %slice.87), kind=kOutput, calls=%fused_computation.17 | convolution fusion | flops 5466488832 | bytes 21270528 | tf_op jit(solution)/shard_map/dot_general | solution.py:45
  335.1 16.0 %convert_reduce_fusion = (f32[4608]{0:T(1024)}, bf16[4,128,4608]{2,1,0:T(8,128)(2,1)}) fusion(f32[4,128,4608]{2,1,0:T(8,128)} %fusion.89, f32[4608]{0:T(1024)S(1)} %slice.87, bf16[4608,1152,1]{1,0,2:T(8,128)(2,1)S(1)} %bitcast.286, bf16[4,128,1152]{2,1,0:T(8,128)(2,1)} %param.23, f32[4,1152]{1,0:T(4,128)S(1)} %get-tuple-element.71), kind=kOutput, calls=%fused_computation.30 | convolution fusion | flops 5489487360 | bytes 26007552 | tf_op jit(solution)/shard_map/dot_general | solution.py:32
  351.0 13.3 %multiply_reduce_fusion.1 = (f32[4,1152]{1,0:T(4,128)}, f32[4,128]{1,0:T(4,128)S(1)}, f32[4,128]{1,0:T(4,128)S(1)}, f32[4,1152]{1,0:T(4,128)}, f32[4,128,1152]{2,1,0:T(8,128)}) fusion(f32[4,128,1152]{2,1,0:T(8,128)S(1)} %copy-done.15, f32[4,128]{1,0:T(4,128)S(1)} %add_rsqrt_fusion, f32[4,128]{1,0:T(4,128)S(1)} %broadcast_multiply_fusion.12, ...), kind=kOutput, calls=%fused_computation.101 | convolution fusion | flops 5441116160 | bytes 20117504 | tf_op jit(solution)/shard_map/dot_general | solution.py:38
  364.3 14.5 %convert_reduce_fusion.2 = (f32[1152]{0:T(1024)}, f32[4,1152]{1,0:T(4,128)}, bf16[4,128,1152]{2,1,0:T(8,128)(2,1)}, f32[4,1152]{1,0:T(4,128)}, f32[4,128,1152]{2,1,0:T(8,128)}) fusion(bf16[4,128,1152]{2,1,0:T(8,128)(2,1)} %param.23, f32[4,1152]{1,0:T(4,128)S(1)} %get-tuple-element.71, f32[4,128,1152]{2,1,0:T(8,128)S(1)} %copy-done.15, ...), kind=kOutput, calls=%fused_computation.99 | convolution fusion | flops 5471787008 | bytes 31960064 | tf_op jit(solution)/shard_map/dot_general | solution.py:38
  386.2 11.5 %fusion.1 = bf16[4608,1152]{1,0:T(8,128)(2,1)} fusion(bf16[4,128,4608]{2,1,0:T(8,128)(2,1)} %get-tuple-element.95, f32[4,128,1152]{2,1,0:T(8,128)} %copy-done.14, f32[4,1152]{1,0:T(4,128)S(1)} %get-tuple-element.72, f32[4,1152]{1,0:T(4,128)S(1)} %get-tuple-element.73, f32[4,128]{1,0:T(4,128)S(1)} %add_rsqrt_fusion, f32[4,128]{1,0:T(4,128)S(1)} %broadcast_multiply_fusion.12), kind=kOutput, calls=%fused_computation.16 | convolution fusion | flops 5444075520 | bytes 17735680 | tf_op jit(solution)/shard_map/dot_general | solution.py:45
  452.1 9.7 %fusion.21 = bf16[4,128,1,1152]{3,1,0,2:T(8,128)(2,1)} fusion(bf16[4,16,8,3456]{3,2,1,0:T(8,128)(2,1)S(1)} %constant_dynamic-update-slice_fusion, bf16[3456,1152,1,1]{1,0,3,2:T(8,128)(2,1)} %bitcast.293), kind=kOutput, calls=%fused_computation.80 | convolution fusion | flops 4077453312 | bytes 12681216 | tf_op jit(solution)/shard_map/dot_general | solution.py:38
  461.8 7.3 fusion.3
  475.3 21.6 %pad_maximum_fusion = bf16[432,32,1152]{2,1,0:T(8,128)(2,1)} fusion(bf16[144,32,1152]{2,1,0:T(8,128)(2,1)} %bitcast.290, bf16[144,32,1152]{2,1,0:T(8,128)(2,1)} %bitcast.291, bf16[36,32,1152]{2,1,0:T(8,128)(2,1)S(1)} %bitcast.298, bf16[108,32,1152]{2,1,0:T(8,128)(2,1)} %bitcast.294), kind=kLoop, calls=%fused_computation.13 | loop fusion | flops 47775744 | bytes 63700992 | tf_op jit(solution)/shard_map/concatenate | solution.py:392
  496.8 10.9 %gather_fusion.9 = bf16[224,16,1152]{2,1,0:T(8,128)(2,1)} fusion(bf16[864,16,1152]{2,1,0:T(8,128)(2,1)} %bitcast.266, s32[1024]{0:T(1024)} %pad_clamp_fusion), kind=kCustom, calls=%fused_computation.9 | custom fusion | bytes 16515968 | tf_op jit(solution)/shard_map/gather | solution.py:407
  516.5 10.8 %gather_fusion.8 = bf16[224,16,1152]{2,1,0:T(8,128)(2,1)} fusion(bf16[864,16,1152]{2,1,0:T(8,128)(2,1)} %bitcast.267, s32[1024]{0:T(1024)} %pad_clamp_fusion.1), kind=kCustom, calls=%fused_computation.8 | custom fusion | bytes 16515968 | tf_op jit(solution)/shard_map/gather | solution.py:407
  535.9 11.3 %gather_fusion.7 = bf16[224,16,1152]{2,1,0:T(8,128)(2,1)} fusion(bf16[864,16,1152]{2,1,0:T(8,128)(2,1)} %bitcast.268, s32[1024]{0:T(1024)} %pad_clamp_fusion.2), kind=kCustom, calls=%fused_computation.7 | custom fusion | bytes 16515968 | tf_op jit(solution)/shard_map/gather | solution.py:407
  547.3 7.6 constant_dynamic-slice_fusion.5
  558.3 10.9 %gather_fusion.6 = bf16[224,16,1152]{2,1,0:T(8,128)(2,1)} fusion(bf16[864,16,1152]{2,1,0:T(8,128)(2,1)} %bitcast.269, s32[1024]{0:T(1024)} %pad_clamp_fusion.3), kind=kCustom, calls=%fused_computation.6 | custom fusion | bytes 16515968 | tf_op jit(solution)/shard_map/gather | solution.py:407
  589.0 8.3 all-to-all-done.6
  603.3 10.0 %all-to-all-done.7 = f32[32,9,128]{2,1,0:T(8,128)S(1)} async-done(((f32[32,9,128]{2,1,0:T(8,128)}), f32[32,9,128]{2,1,0:T(8,128)S(1)}, u32[]{:S(2)}, u32[]{:S(2)}) %all-to-all-start.7) | async-done | bytes 147488 | tf_op jit(solution)/shard_map/all_to_all | solution.py:77
  656.2 7.2 convert_add_fusion.2
  672.2 18.7 %collective-permute-done.16 = bf16[2,2,2,7,16,1152]{5,4,3,1,2,0:T(8,128)(2,1)} collective-permute-done((bf16[2,2,2,7,16,1152]{5,4,3,1,2,0:T(8,128)(2,1)S(1)}, bf16[2,2,2,7,16,1152]{5,4,3,1,2,0:T(8,128)(2,1)}, u32[]{:S(2)}, u32[]{:S(2)}) %collective-permute-start.16) | collective-permute-done | bytes 2064416 | tf_op jit(solution)/shard_map/ppermute | solution.py:104
  707.5 27.6 %collective-permute-done.6 = bf16[2,2,2,7,16,1152]{5,4,3,1,2,0:T(8,128)(2,1)} collective-permute-done((bf16[2,2,2,7,16,1152]{5,4,3,1,2,0:T(8,128)(2,1)}, bf16[2,2,2,7,16,1152]{5,4,3,1,2,0:T(8,128)(2,1)}, u32[]{:S(2)}, u32[]{:S(2)}) %collective-permute-start.6) | collective-permute-done | bytes 2064416 | tf_op jit(solution)/shard_map/ppermute | solution.py:104
  748.2 18.8 %collective-permute-done.17 = bf16[2,2,7,16,1152]{4,3,2,0,1:T(8,128)(2,1)} collective-permute-done((bf16[2,2,7,16,1152]{4,3,2,0,1:T(8,128)(2,1)S(1)}, bf16[2,2,7,16,1152]{4,3,2,0,1:T(8,128)(2,1)}, u32[]{:S(2)}, u32[]{:S(2)}) %collective-permute-start.17) | collective-permute-done | bytes 1032224 | tf_op jit(solution)/shard_map/ppermute | solution.py:104
  772.2 16.2 %collective-permute-done.7 = bf16[2,2,7,16,1152]{4,3,2,0,1:T(8,128)(2,1)S(1)} collective-permute-done((bf16[2,2,7,16,1152]{4,3,2,0,1:T(8,128)(2,1)S(1)}, bf16[2,2,7,16,1152]{4,3,2,0,1:T(8,128)(2,1)S(1)}, u32[]{:S(2)}, u32[]{:S(2)}) %collective-permute-start.7) | collective-permute-done | bytes 1032224 | tf_op jit(solution)/shard_map/ppermute | solution.py:104
  794.8 20.8 %collective-permute-done.8 = bf16[2,7,16,1152]{3,2,1,0:T(8,128)(2,1)S(1)} collective-permute-done((bf16[2,7,16,1152]{3,2,1,0:T(8,128)(2,1)S(1)}, bf16[2,7,16,1152]{3,2,1,0:T(8,128)(2,1)S(1)}, u32[]{:S(2)}, u32[]{:S(2)}) %collective-permute-start.8) | collective-permute-done | bytes 516128 | tf_op jit(solution)/shard_map/ppermute | solution.py:104
  815.9 9.6 %collective-permute-done.3 = bf16[2,7,16,1152]{3,2,1,0:T(8,128)(2,1)S(1)} collective-permute-done((bf16[2,7,16,1152]{3,2,1,0:T(8,128)(2,1)S(1)}, bf16[2,7,16,1152]{3,2,1,0:T(8,128)(2,1)S(1)}, u32[]{:S(2)}, u32[]{:S(2)}) %collective-permute-start.3) | collective-permute-done | bytes 516128 | tf_op jit(solution)/shard_map/ppermute | solution.py:104
  825.9 16.5 %collective-permute-done.9 = bf16[7,16,1152]{2,1,0:T(8,128)(2,1)S(1)} collective-permute-done((bf16[7,16,1152]{2,1,0:T(8,128)(2,1)S(1)}, bf16[7,16,1152]{2,1,0:T(8,128)(2,1)S(1)}, u32[]{:S(2)}, u32[]{:S(2)}) %collective-permute-start.9) | collective-permute-done | bytes 258080 | tf_op jit(solution)/shard_map/ppermute | solution.py:104
  862.5 7.1 fusion.100
  (398 shorter events, 313.9 us)
Async XLA Ops:
  7.2 207.9 %all-gather.2.cloned.1.call-start = ((), (), s32[]{:S(2)}) async-start(), calls=%async_computation.10 | async-start | bytes 34062336 | tf_op jit(solution)/shard_map/all_gather | solution.py:176
  9.3 15.4 %all-to-all-start = ((bf16[4,4,1152]{2,1,0:T(4,128)(2,1)}), bf16[4,4,1152]{2,1,0:T(4,128)(2,1)S(1)}, u32[]{:S(2)}, u32[]{:S(2)}) async-start(bf16[4,4,1152]{2,1,0:T(4,128)(2,1)} %tile.2), calls=%async_computation | async-start | bytes 73728 | tf_op jit(solution)/shard_map/all_to_all | solution.py:195
  25.7 16.3 %all-to-all-start.1 = ((f32[32,4,224]{2,1,0:T(4,128)}), f32[32,4,224]{2,1,0:T(4,128)S(1)}, u32[]{:S(2)}, u32[]{:S(2)}) async-start(f32[32,4,224]{2,1,0:T(4,128)} %bitcast.2), calls=%async_computation.1 | async-start | bytes 262144 | tf_op jit(solution)/shard_map/all_to_all | solution.py:201
  45.7 27.7 %all-to-all-start.2 = ((bf16[4,16,8,1152]{3,1,0,2:T(8,128)(2,1)}), bf16[4,16,8,1152]{3,1,0,2:T(8,128)(2,1)S(1)}, u32[]{:S(2)}, u32[]{:S(2)}) async-start(bf16[4,16,8,1152]{3,1,0,2:T(8,128)(2,1)} %copy.180), calls=%async_computation.2 | async-start | bytes 2359296 | tf_op jit(solution)/shard_map/all_to_all | solution.py:221
  275.3 30.6 %all-to-all-start.3 = ((bf16[4,128,1,1152]{3,0,2,1:T(4,128)(2,1)}), bf16[4,128,1,1152]{3,0,2,1:T(4,128)(2,1)S(1)}, u32[]{:S(2)}, u32[]{:S(2)}) async-start(bf16[4,128,1,1152]{3,0,2,1:T(4,128)(2,1)} %copy.188), calls=%async_computation.3 | async-start | bytes 2359296 | tf_op jit(solution)/shard_map/all_to_all | solution.py:256
  381.8 21.2 %all-to-all-start.4 = ((bf16[4,16,8,1152]{3,1,0,2:T(8,128)(2,1)}), bf16[4,16,8,1152]{3,1,0,2:T(8,128)(2,1)S(1)}, u32[]{:S(2)}, u32[]{:S(2)}) async-start(bf16[4,16,8,1152]{3,1,0,2:T(8,128)(2,1)} %copy.190), calls=%async_computation.4 | async-start | bytes 2359296 | tf_op jit(solution)/shard_map/all_to_all | solution.py:286
  471.0 107.6 %all-to-all-start.5 = ((bf16[4,128,1,1152]{3,0,2,1:T(4,128)(2,1)}), bf16[4,128,1,1152]{3,0,2,1:T(4,128)(2,1)}, u32[]{:S(2)}, u32[]{:S(2)}) async-start(bf16[4,128,1,1152]{3,0,2,1:T(4,128)(2,1)} %copy.201), calls=%async_computation.5 | async-start | bytes 2359296 | tf_op jit(solution)/shard_map/all_to_all | solution.py:324
  516.1 122.0 %collective-permute-start.15 = (bf16[2,2,2,2,7,16,1152]{6,5,4,2,3,1,0:T(8,128)(2,1)}, bf16[2,2,2,2,7,16,1152]{6,5,4,2,3,1,0:T(8,128)(2,1)}, u32[]{:S(2)}, u32[]{:S(2)}) collective-permute-start(bf16[2,2,2,2,7,16,1152]{6,5,4,2,3,1,0:T(8,128)(2,1)} %bitcast.257), channel_id=1, source_target_pairs={{0,4},{4,0},{8,12},{12,8},{16,20},{20,16},{24,28},{28,24},{1,5},{5... | collective-permute-start | bytes 12386312 | tf_op jit(solution)/shard_map/ppermute | solution.py:104
  535.8 108.2 %collective-permute-start.10 = (bf16[2,2,2,2,7,16,1152]{6,5,4,2,3,0,1:T(8,128)(2,1)}, bf16[2,2,2,2,7,16,1152]{6,5,4,2,3,0,1:T(8,128)(2,1)}, u32[]{:S(2)}, u32[]{:S(2)}) collective-permute-start(bf16[2,2,2,2,7,16,1152]{6,5,4,2,3,0,1:T(8,128)(2,1)} %bitcast.258), channel_id=1, source_target_pairs={{0,4},{4,0},{8,12},{12,8},{16,20},{20,16},{24,28},{28,24},{1,5},{5... | collective-permute-start | bytes 12386312 | tf_op jit(solution)/shard_map/ppermute | solution.py:104
  573.9 79.6 %collective-permute-start.5 = (bf16[2,2,2,2,7,16,1152]{6,5,4,2,3,1,0:T(8,128)(2,1)}, bf16[2,2,2,2,7,16,1152]{6,5,4,2,3,1,0:T(8,128)(2,1)}, u32[]{:S(2)}, u32[]{:S(2)}) collective-permute-start(bf16[2,2,2,2,7,16,1152]{6,5,4,2,3,1,0:T(8,128)(2,1)} %bitcast.259), channel_id=1, source_target_pairs={{0,4},{4,0},{8,12},{12,8},{16,20},{20,16},{24,28},{28,24},{1,5},{5... | collective-permute-start | bytes 12386312 | tf_op jit(solution)/shard_map/ppermute | solution.py:104
  577.7 90.4 %collective-permute-start = (bf16[2,2,2,2,7,16,1152]{6,5,4,3,2,1,0:T(8,128)(2,1)}, bf16[2,2,2,2,7,16,1152]{6,5,4,3,2,1,0:T(8,128)(2,1)}, u32[]{:S(2)}, u32[]{:S(2)}) collective-permute-start(bf16[2,2,2,2,7,16,1152]{6,5,4,3,2,1,0:T(8,128)(2,1)} %dynamic-slice_bitcast_fusion), channel_id=1, source_target_pairs={{0,4},{4,0},{8,12},{12,8},{16,20},{20,16},{24,28},{28,24},{1,5},{5... | collective-permute-start | bytes 12386312 | tf_op jit(solution)/shard_map/ppermute | solution.py:104
  585.0 12.3 %all-to-all-start.6 = ((f32[32,4,224]{2,1,0:T(4,128)}), f32[32,4,224]{2,1,0:T(4,128)S(1)}, u32[]{:S(2)}, u32[]{:S(2)}) async-start(f32[32,4,224]{2,1,0:T(4,128)} %reshape.532), calls=%async_computation.6 | async-start | bytes 262144 | tf_op jit(solution)/shard_map/all_to_all | solution.py:356
  600.5 12.8 %all-to-all-start.7 = ((f32[32,9,128]{2,1,0:T(8,128)}), f32[32,9,128]{2,1,0:T(8,128)S(1)}, u32[]{:S(2)}, u32[]{:S(2)}) async-start(f32[32,9,128]{2,1,0:T(8,128)} %reshape.399), calls=%async_computation.7 | async-start | bytes 524288 | tf_op jit(solution)/shard_map/all_to_all | solution.py:77
  614.1 12.9 %all-to-all-start.8 = ((f32[32,9,128]{2,1,0:T(8,128)}), f32[32,9,128]{2,1,0:T(8,128)S(1)}, u32[]{:S(2)}, u32[]{:S(2)}) async-start(f32[32,9,128]{2,1,0:T(8,128)} %broadcast_in_dim.131), calls=%async_computation.8 | async-start | bytes 524288 | tf_op jit(solution)/shard_map/all_to_all | solution.py:77
  642.9 48.0 %collective-permute-start.16 = (bf16[2,2,2,7,16,1152]{5,4,3,1,2,0:T(8,128)(2,1)S(1)}, bf16[2,2,2,7,16,1152]{5,4,3,1,2,0:T(8,128)(2,1)}, u32[]{:S(2)}, u32[]{:S(2)}) collective-permute-start(bf16[2,2,2,7,16,1152]{5,4,3,1,2,0:T(8,128)(2,1)S(1)} %fusion.41), channel_id=1, source_target_pairs={{0,16},{4,20},{8,24},{12,28},{16,0},{20,4},{24,8},{28,12},{1,17},{... | collective-permute-start | bytes 6193160 | tf_op jit(solution)/shard_map/ppermute | solution.py:104
  652.6 48.1 %collective-permute-start.11 = (bf16[2,2,2,7,16,1152]{5,4,3,1,2,0:T(8,128)(2,1)}, bf16[2,2,2,7,16,1152]{5,4,3,1,2,0:T(8,128)(2,1)}, u32[]{:S(2)}, u32[]{:S(2)}) collective-permute-start(bf16[2,2,2,7,16,1152]{5,4,3,1,2,0:T(8,128)(2,1)} %fusion.40), channel_id=1, source_target_pairs={{0,8},{4,12},{8,0},{12,4},{16,24},{20,28},{24,16},{28,20},{1,9},{5... | collective-permute-start | bytes 6193160 | tf_op jit(solution)/shard_map/ppermute | solution.py:104
  667.1 68.0 %collective-permute-start.6 = (bf16[2,2,2,7,16,1152]{5,4,3,1,2,0:T(8,128)(2,1)}, bf16[2,2,2,7,16,1152]{5,4,3,1,2,0:T(8,128)(2,1)}, u32[]{:S(2)}, u32[]{:S(2)}) collective-permute-start(bf16[2,2,2,7,16,1152]{5,4,3,1,2,0:T(8,128)(2,1)} %fusion.39), channel_id=1, source_target_pairs={{0,16},{4,20},{8,24},{12,28},{16,0},{20,4},{24,8},{28,12},{1,17},{... | collective-permute-start | bytes 6193160 | tf_op jit(solution)/shard_map/ppermute | solution.py:104
  671.6 73.3 %collective-permute-start.1 = (bf16[2,2,2,7,16,1152]{5,4,3,2,1,0:T(8,128)(2,1)S(1)}, bf16[2,2,2,7,16,1152]{5,4,3,2,1,0:T(8,128)(2,1)}, u32[]{:S(2)}, u32[]{:S(2)}) collective-permute-start(bf16[2,2,2,7,16,1152]{5,4,3,2,1,0:T(8,128)(2,1)S(1)} %fusion.38), channel_id=1, source_target_pairs={{0,8},{4,12},{8,0},{12,4},{16,24},{20,28},{24,16},{28,20},{1,9},{5... | collective-permute-start | bytes 6193160 | tf_op jit(solution)/shard_map/ppermute | solution.py:104
  690.9 44.2 %slice-start.4 = ((s8[8257536]{0:T(1024)(128)(4,1)}), s8[4194304]{0:T(1024)(128)(4,1)S(1)}, s32[]{:S(2)}) async-start(s8[8257536]{0:T(1024)(128)(4,1)} %bitcast.279), calls=%async_computation.15 | async-start | bytes 8388608
  694.3 72.7 %collective-permute-start.17 = (bf16[2,2,7,16,1152]{4,3,2,0,1:T(8,128)(2,1)S(1)}, bf16[2,2,7,16,1152]{4,3,2,0,1:T(8,128)(2,1)}, u32[]{:S(2)}, u32[]{:S(2)}) collective-permute-start(bf16[2,2,7,16,1152]{4,3,2,0,1:T(8,128)(2,1)S(1)} %fusion.67), channel_id=1, source_target_pairs={{0,8},{4,12},{8,0},{12,4},{16,24},{20,28},{24,16},{28,20},{1,9},{5... | collective-permute-start | bytes 3096584 | tf_op jit(solution)/shard_map/ppermute | solution.py:104
  706.4 62.9 %collective-permute-start.12 = (bf16[2,2,7,16,1152]{4,3,2,0,1:T(8,128)(2,1)S(1)}, bf16[2,2,7,16,1152]{4,3,2,0,1:T(8,128)(2,1)}, u32[]{:S(2)}, u32[]{:S(2)}) collective-permute-start(bf16[2,2,7,16,1152]{4,3,2,0,1:T(8,128)(2,1)S(1)} %fusion.66), channel_id=1, source_target_pairs={{0,16},{4,20},{8,24},{12,28},{16,0},{20,4},{24,8},{28,12},{1,17},{... | collective-permute-start | bytes 3096584 | tf_op jit(solution)/shard_map/ppermute | solution.py:104
  737.3 51.1 %collective-permute-start.7 = (bf16[2,2,7,16,1152]{4,3,2,0,1:T(8,128)(2,1)S(1)}, bf16[2,2,7,16,1152]{4,3,2,0,1:T(8,128)(2,1)S(1)}, u32[]{:S(2)}, u32[]{:S(2)}) collective-permute-start(bf16[2,2,7,16,1152]{4,3,2,0,1:T(8,128)(2,1)S(1)} %fusion.65), channel_id=1, source_target_pairs={{0,8},{4,12},{8,0},{12,4},{16,24},{20,28},{24,16},{28,20},{1,9},{5... | collective-permute-start | bytes 3096584 | tf_op jit(solution)/shard_map/ppermute | solution.py:104
  747.1 41.6 %collective-permute-start.2 = (bf16[2,2,7,16,1152]{4,3,2,1,0:T(8,128)(2,1)S(1)}, bf16[2,2,7,16,1152]{4,3,2,1,0:T(8,128)(2,1)S(1)}, u32[]{:S(2)}, u32[]{:S(2)}) collective-permute-start(bf16[2,2,7,16,1152]{4,3,2,1,0:T(8,128)(2,1)S(1)} %fusion.64), channel_id=1, source_target_pairs={{0,16},{4,20},{8,24},{12,28},{16,0},{20,4},{24,8},{28,12},{1,17},{... | collective-permute-start | bytes 3096584 | tf_op jit(solution)/shard_map/ppermute | solution.py:104
  768.5 22.6 %collective-permute-start.18 = (bf16[2,7,16,1152]{3,2,1,0:T(8,128)(2,1)S(1)}, bf16[2,7,16,1152]{3,2,1,0:T(8,128)(2,1)S(1)}, u32[]{:S(2)}, u32[]{:S(2)}) collective-permute-start(bf16[2,7,16,1152]{3,2,1,0:T(8,128)(2,1)S(1)} %fusion.73), channel_id=1, source_target_pairs={{0,1},{1,0},{2,3},{3,2},{4,5},{5,4},{6,7},{7,6},{8,9},{9,8},{10,11... | collective-permute-start | bytes 1548296 | tf_op jit(solution)/shard_map/ppermute | solution.py:104
  770.8 22.7 %collective-permute-start.13 = (bf16[2,7,16,1152]{3,2,1,0:T(8,128)(2,1)S(1)}, bf16[2,7,16,1152]{3,2,1,0:T(8,128)(2,1)S(1)}, u32[]{:S(2)}, u32[]{:S(2)}) collective-permute-start(bf16[2,7,16,1152]{3,2,1,0:T(8,128)(2,1)S(1)} %fusion.72), channel_id=1, source_target_pairs={{0,1},{1,0},{2,3},{3,2},{4,5},{5,4},{6,7},{7,6},{8,9},{9,8},{10,11... | collective-permute-start | bytes 1548296 | tf_op jit(solution)/shard_map/ppermute | solution.py:104
  788.7 27.0 %collective-permute-start.8 = (bf16[2,7,16,1152]{3,2,1,0:T(8,128)(2,1)S(1)}, bf16[2,7,16,1152]{3,2,1,0:T(8,128)(2,1)S(1)}, u32[]{:S(2)}, u32[]{:S(2)}) collective-permute-start(bf16[2,7,16,1152]{3,2,1,0:T(8,128)(2,1)S(1)} %fusion.71), channel_id=1, source_target_pairs={{0,1},{1,0},{2,3},{3,2},{4,5},{5,4},{6,7},{7,6},{8,9},{9,8},{10,11... | collective-permute-start | bytes 1548296 | tf_op jit(solution)/shard_map/ppermute | solution.py:104
  789.0 36.4 %collective-permute-start.3 = (bf16[2,7,16,1152]{3,2,1,0:T(8,128)(2,1)S(1)}, bf16[2,7,16,1152]{3,2,1,0:T(8,128)(2,1)S(1)}, u32[]{:S(2)}, u32[]{:S(2)}) collective-permute-start(bf16[2,7,16,1152]{3,2,1,0:T(8,128)(2,1)S(1)} %fusion.70), channel_id=1, source_target_pairs={{0,1},{1,0},{2,3},{3,2},{4,5},{5,4},{6,7},{7,6},{8,9},{9,8},{10,11... | collective-permute-start | bytes 1548296 | tf_op jit(solution)/shard_map/ppermute | solution.py:104
  791.3 34.4 %collective-permute-start.19 = (bf16[7,16,1152]{2,1,0:T(8,128)(2,1)S(1)}, bf16[7,16,1152]{2,1,0:T(8,128)(2,1)S(1)}, u32[]{:S(2)}, u32[]{:S(2)}) collective-permute-start(bf16[7,16,1152]{2,1,0:T(8,128)(2,1)S(1)} %fusion.77), channel_id=1, source_target_pairs={{0,2},{1,3},{2,0},{3,1},{4,6},{5,7},{6,4},{7,5},{8,10},{9,11},{10,... | collective-permute-start | bytes 774152 | tf_op jit(solution)/shard_map/ppermute | solution.py:104
  793.7 32.1 %collective-permute-start.14 = (bf16[7,16,1152]{2,1,0:T(8,128)(2,1)S(1)}, bf16[7,16,1152]{2,1,0:T(8,128)(2,1)S(1)}, u32[]{:S(2)}, u32[]{:S(2)}) collective-permute-start(bf16[7,16,1152]{2,1,0:T(8,128)(2,1)S(1)} %fusion.76), channel_id=1, source_target_pairs={{0,2},{1,3},{2,0},{3,1},{4,6},{5,7},{6,4},{7,5},{8,10},{9,11},{10,... | collective-permute-start | bytes 774152 | tf_op jit(solution)/shard_map/ppermute | solution.py:104
  815.8 26.6 %collective-permute-start.9 = (bf16[7,16,1152]{2,1,0:T(8,128)(2,1)S(1)}, bf16[7,16,1152]{2,1,0:T(8,128)(2,1)S(1)}, u32[]{:S(2)}, u32[]{:S(2)}) collective-permute-start(bf16[7,16,1152]{2,1,0:T(8,128)(2,1)S(1)} %fusion.75), channel_id=1, source_target_pairs={{0,2},{1,3},{2,0},{3,1},{4,6},{5,7},{6,4},{7,5},{8,10},{9,11},{10,... | collective-permute-start | bytes 774152 | tf_op jit(solution)/shard_map/ppermute | solution.py:104
  825.6 22.2 %collective-permute-start.4 = (bf16[7,16,1152]{2,1,0:T(8,128)(2,1)S(1)}, bf16[7,16,1152]{2,1,0:T(8,128)(2,1)S(1)}, u32[]{:S(2)}, u32[]{:S(2)}) collective-permute-start(bf16[7,16,1152]{2,1,0:T(8,128)(2,1)S(1)} %fusion.74), channel_id=1, source_target_pairs={{0,2},{1,3},{2,0},{3,1},{4,6},{5,7},{6,4},{7,5},{8,10},{9,11},{10,... | collective-permute-start | bytes 774152 | tf_op jit(solution)/shard_map/ppermute | solution.py:104
  851.4 9.7 %all-to-all-start.9 = ((f32[32,1,128]{2,1,0:T(1,128)}), f32[32,1,128]{2,1,0:T(1,128)S(1)}, u32[]{:S(2)}, u32[]{:S(2)}) async-start(f32[32,1,128]{2,1,0:T(1,128)} %broadcast_in_dim.136), calls=%async_computation.9 | async-start | bytes 32768 | tf_op jit(solution)/shard_map/all_to_all | solution.py:77
  (73 other events, 708.6 us)
Sparse Core Ops, SparseCore 0:
  10.8 204.2 all-gather.1
